TPU v7x, 32 devices: a whole 2x2x4 slice. The times are simulated.
32 devices in a mesh: gx: 8 (over z, y), gy: 4 (over x, core).
Axes of the slice: x: 2, y: 2, z: 4, core: 2. Of those that a mesh axis runs over, the one named last changes fastest.
Arguments:
- layer_in: bfloat16 [2048, 1536], P('gx', 'gy'), may hold values from -40 to 40
- first_gain: float32 [1536], P('gy'), may hold values from 0.5 to 1.5
- query_weight: bfloat16 [1536, 1536], P('gx', 'gy'), may hold values from -0.21875 to 0.21875
- key_matrix: bfloat16 [1536, 768], P('gx', 'gy'), may hold values from -0.21875 to 0.21875
- value_matrix: bfloat16 [1536, 768], P('gx', 'gy'), may hold values from -0.15625 to 0.15625
- out_weight: bfloat16 [1536, 1536], P('gy', 'gx'), may hold values from -0.875 to 0.875
- second_gain: float32 [1536], P('gy'), may hold values from 0.5 to 1.5
- gate_weight: bfloat16 [1536, 4096], P('gx', 'gy'), may hold values from -0.15625 to 0.15625
- up_weight: bfloat16 [1536, 4096], P('gx', 'gy'), may hold values from -0.15625 to 0.15625
- down_weight: bfloat16 [4096, 1536], P('gy', 'gx'), may hold values from -0.1875 to 0.1875
- out_grad: bfloat16 [2048, 1536], P('gx', 'gy'), may hold values from -6 to 6
Outputs:
- layer_out: bfloat16 [2048, 1536], P('gx', 'gy')
- in_grad: float32 [2048, 1536], P('gx', 'gy')
- first_gain_grad: float32 [1536], P('gy')
- query_grad: float32 [1536, 1536], P('gx', 'gy')
- key_grad: float32 [1536, 768], P('gx', 'gy')
- value_grad: float32 [1536, 768], P('gx', 'gy')
- out_proj_grad: float32 [1536, 1536], P('gy', 'gx')
- second_gain_grad: float32 [1536], P('gy')
- gate_grad: float32 [1536, 4096], P('gx', 'gy')
- up_grad: float32 [1536, 4096], P('gx', 'gy')
- down_grad: float32 [4096, 1536], P('gy', 'gx')
All inputs are finite; a program needn't handle non-finite values.
Results may differ from a plain program's by a relative error of at most 0.024.
Values may be sent and summed in bfloat16 or wider, within the bound.
No kernel may reach another device: no remote copies, remote signals or barrier semaphores. Data moves between devices by JAX's collectives and lax.ppermute only.
A program may use at most 128 MiB of HBM per device.

v0:
```python
import jax
import jax.numpy as jnp
from jax import lax
from jax.experimental import pallas as pl
from jax.experimental.pallas import tpu as pltpu
from jax.sharding import PartitionSpec as P

HEAD_DIM = 96
PROMPT_DEV = 4
CONT_DEV = 4
GROUP = (PROMPT_DEV + CONT_DEV) // 2
PROMPTS = PROMPT_DEV // 2

eps = 1e-05
neg_big = -1e30
rope_base = 100000.0
score_scale = HEAD_DIM ** (-0.5)
f32 = jnp.float32
bf16 = jnp.bfloat16


def dims(left, right, left_axis, right_axis):
    return lax.dot_general(
        left, right, (((left_axis,), (right_axis,)), ((), ())), preferred_element_type=f32
    )


class Place:
    def __init__(self):
        self.nx = lax.axis_size("gx")
        self.ny = lax.axis_size("gy")
        assert self.ny == 4 and self.nx % (PROMPT_DEV + CONT_DEV) == 0
        self.n = self.nx // 2
        self.gx = lax.axis_index("gx")
        self.gy = lax.axis_index("gy")
        self.z, self.y = self.gx // 2, self.gx % 2
        self.x, self.c = self.gy // 2, self.gy % 2
        self.z_in = self.z % GROUP
        offset = 2 * self.z_in + jnp.arange(2, dtype=jnp.int32)
        self.offset = offset
        self.lined = self.n == self.ny
        blocks = jnp.arange(self.ny, dtype=jnp.int32)
        first = jnp.stack([self.z, self.y, self.x, self.c, self.z_in]).astype(jnp.int32)
        self.table = jnp.concatenate(
            [first, jnp.minimum(offset, PROMPT_DEV), blocks ^ self.z if self.lined else blocks]
        )

    def swap_gx(self, value, bit):
        return lax.ppermute(value, "gx", [(i, i ^ bit) for i in range(self.nx)])

    def swap_y(self, value):
        return self.swap_gx(value, 1)

    def swap_x(self, value):
        return lax.ppermute(value, "gy", [(i, i ^ 2) for i in range(self.ny)])

    def swap_c(self, value):
        return lax.ppermute(value, "gy", [(i, i ^ 1) for i in range(self.ny)])

    def send_z(self, value, moves):
        pairs = [(2 * s + y, 2 * t + y) for s, t in moves for y in range(2)]
        return lax.ppermute(value, "gx", pairs)

    def by_y(self):
        return [[2 * z + y for z in range(self.n)] for y in range(2)]


def pair(flag, mine, other):
    return jnp.where(flag == 0, mine, other), jnp.where(flag == 0, other, mine)


def part_of(flag, whole, axis):
    low, high = jnp.split(whole, 2, axis)
    return jnp.where(flag == 0, low, high), jnp.where(flag == 0, high, low)


def after(value, *earlier):
    return lax.optimization_barrier((value,) + earlier)[0]


NEAR = [(0, 1), (1, 0), (2, 3), (3, 2)]
SECOND = [(0, 2), (1, 3), (2, 0), (3, 1)]
MIDDLE = [(1, 2), (2, 1)]
INWARD = [(0, 1), (3, 2)]
OUTWARD = [(1, 0), (2, 3)]


def gather_pieces(place, piece):
    near = place.send_z(piece, NEAR)
    second = place.send_z(piece, SECOND)
    middle = place.send_z(piece, MIDDLE)
    return [piece, near, second, middle, place.send_z(second, OUTWARD)]


def gather_whole(place, piece, by_rows):
    every = lax.all_gather(piece, "gx", axis_index_groups=place.by_y())
    inner = place.n // place.ny
    rows, cols = piece.shape
    if by_rows:
        return every.reshape(place.ny, inner * rows, cols)
    every = every.reshape(place.ny, inner, rows, cols)
    return jnp.swapaxes(every, 1, 2).reshape(place.ny, rows, inner * cols)


def scatter_sum(place, parts, by_rows):
    if not place.lined:
        n = place.n
        inner = n // place.ny
        parts = jnp.stack(parts)
        count, rows, cols = parts.shape
        if by_rows:
            parts = parts.reshape(n, rows // inner, cols)
        else:
            parts = jnp.swapaxes(parts.reshape(count, rows, inner, cols // inner), 1, 2)
            parts = parts.reshape(n, rows, cols // inner)
        return lax.psum_scatter(parts, "gx", axis_index_groups=place.by_y()).astype(f32)
    own, near, second, third = parts
    far = place.send_z(third, INWARD)
    near = place.send_z(near, NEAR)
    middle = place.send_z(third, MIDDLE)
    second = place.send_z((second.astype(f32) + far.astype(f32)).astype(bf16), SECOND)
    return own.astype(f32) + near.astype(f32) + middle.astype(f32) + second.astype(f32)


def all_sum(place, keep, send, *earlier):
    got = place.swap_c(send)
    first, second = keep[0] + got[0].astype(f32), keep[1] + got[1].astype(f32)
    first_got = place.swap_x(first.astype(bf16))
    second_got = place.swap_y(second.astype(bf16))
    first, second = first + first_got.astype(f32), second + second_got.astype(f32)
    first_low, second_low = first.astype(bf16), second.astype(bf16)
    if earlier:
        first_low, second_low = lax.optimization_barrier((first_low, second_low) + earlier)[:2]
    first_got = place.swap_y(first_low)
    second_got = place.swap_x(second_low)
    own = [
        (first + first_got.astype(f32)).astype(bf16),
        (second + second_got.astype(f32)).astype(bf16),
    ]
    return own + [place.swap_c(part) for part in own]


def own_sum(place, keep, send):
    got = place.swap_c(send)
    first, second = keep[0] + got[0].astype(f32), keep[1] + got[1].astype(f32)
    mine, other = jnp.where(place.x == 0, first, second), jnp.where(place.x == 0, second, first)
    mine = mine + place.swap_x(other.astype(bf16)).astype(f32)
    mine, other = part_of(place.y, mine, 0)
    return mine + place.swap_y(other.astype(bf16)).astype(f32)


def own_block(place, blocks):
    rows = blocks.shape[1] // 2
    return lax.dynamic_slice(
        blocks, (place.gy, place.y * rows, 0), (1, rows, blocks.shape[2])
    )[0]


Z, Y, X, C, Z_IN, COUNT = range(6)
ORDER = COUNT + 2


def call(body, outs, table, operands, pieces=(), scratch=(), earlier=(), limit=24):
    lengths = [len(p) for p in pieces]
    flat = [a for p in pieces for a in p] + list(earlier)
    vmem = pl.BlockSpec(memory_space=pltpu.VMEM)

    def kernel(table_ref, *refs):
        plain, rest = refs[: len(operands)], refs[len(operands) :]
        lists = []
        for length in lengths:
            lists.append(rest[:length])
            rest = rest[length:]
        rest = rest[len(earlier) :]
        body(table_ref, *plain, *lists, *rest)

    return pl.pallas_call(
        kernel,
        out_shape=[jax.ShapeDtypeStruct(shape, dtype) for shape, dtype in outs],
        in_specs=[pl.BlockSpec(memory_space=pltpu.SMEM)]
        + [vmem] * len(operands)
        + [pl.BlockSpec(memory_space=pl.ANY)] * len(flat),
        out_specs=[vmem] * len(outs),
        scratch_shapes=list(scratch),
        compiler_params=pltpu.CompilerParams(vmem_limit_bytes=limit << 20),
    )(table, *operands, *flat)


def start_pieces(table, pieces, whole, sems):
    if len(pieces) == 1:
        copy = pltpu.make_async_copy(pieces[0], whole, sems.at[0])
        copy.start()
        return copy.wait
    z = table[Z]
    own, near, second, middle, end = pieces
    inside = jnp.logical_or(z == 1, z == 2)
    pltpu.make_async_copy(own, whole.at[table[ORDER]], sems.at[0]).start()
    pltpu.make_async_copy(near, whole.at[table[ORDER + 1]], sems.at[1]).start()
    pltpu.make_async_copy(second, whole.at[table[ORDER + 2]], sems.at[2]).start()

    @pl.when(inside)
    def _():
        pltpu.make_async_copy(middle, whole.at[table[ORDER + 3]], sems.at[3]).start()

    @pl.when(jnp.logical_not(inside))
    def _():
        pltpu.make_async_copy(end, whole.at[table[ORDER + 3]], sems.at[3]).start()

    def wait():
        for k in range(4):
            pltpu.make_async_copy(own, whole.at[0], sems.at[k]).wait()

    return wait


def keep_and_send(table, block_of, keep_first, keep_second, send):
    core = table[C]
    keep_first[...] = block_of(core)
    keep_second[...] = block_of(2 + core)

    def one(i, _):
        send[i] = block_of(2 * i + 1 - core).astype(bf16)
        return 0

    lax.fori_loop(0, 2, one, 0)


def place_rows(table, pieces, whole):
    x, y, c = table[X], table[Y], table[C]
    tokens = pieces[0].shape[0]
    for dc in range(2):
        for dx in range(2):
            block = 2 * (x + dx - 2 * x * dx) + c + dc - 2 * c * dc
            for dy in range(2):
                at = pl.ds(pl.multiple_of(tokens * (y + dy - 2 * y * dy), tokens), tokens)
                whole[block, at, :] = pieces[4 * dc + 2 * dy + dx][...]


def grad_body(table, *refs):
    place_rows(table, refs[:8], refs[8])


def rows_body(table, *refs):
    rows, gains = refs[:8], refs[8:12]
    raw, normed, inverse, gain_first, gain_second = refs[12:]
    place_rows(table, rows, raw)
    x, c = table[X], table[C]
    for dc in range(2):
        for dx in range(2):
            block = 2 * (x + dx - 2 * x * dx) + c + dc - 2 * c * dc
            gain = gains[2 * dc + dx][...]
            gain_first[block] = gain[0:1]
            gain_second[block] = gain[1:2]

    def square(b, total):
        values = raw[b].astype(f32)
        return total + jnp.sum(values * values, axis=1, keepdims=True)

    count = raw.shape[0]
    total = lax.fori_loop(0, count, square, jnp.zeros((raw.shape[1], 1), f32))
    scale = lax.rsqrt(total / (count * raw.shape[2]) + eps)
    inverse[...] = scale

    def norm(b, _):
        normed[b] = (raw[b].astype(f32) * scale * gain_first[b]).astype(bf16)
        return 0

    lax.fori_loop(0, count, norm, 0)


def turn(values, cosine, sine):
    half = values.shape[0] // 2
    first, second = values[:half], values[half:]
    return jnp.concatenate(
        [first * cosine - second * sine, second * cosine + first * sine], axis=0
    )


def qkv_body(table, normed, cosine, sine, pieces, query, own, weights, acc, sems):
    start_pieces(table, pieces, weights, sems)()
    model = normed.shape[2]
    acc[...] = jnp.zeros_like(acc)

    def one(b, _):
        acc[...] += dims(normed[b], weights[b, :model], 1, 0)
        return 0

    lax.fori_loop(0, normed.shape[0], one, 0)
    flipped = acc[...].T
    head = HEAD_DIM
    heads = query.shape[0] // head
    cos, sin = cosine[...], sine[...]
    for h in range(heads):
        at = slice(h * head, (h + 1) * head)
        query[at] = turn(flipped[at], cos, sin).astype(bf16)
    at = slice(heads * head, (heads + 1) * head)
    own[:head] = turn(flipped[at], cos, sin).astype(bf16)
    own[head:] = flipped[(heads + 1) * head :].astype(bf16)


def attend_body(
    table, query, own, *refs
):
    moved = refs[: GROUP - 1]
    weights, attended, attended_low, log_total, far, keep_first, keep_second, send = refs[
        GROUP - 1 :
    ]
    tokens = own.shape[1]
    for place in range(GROUP):

        @pl.when(table[Z_IN] == place)
        def _():
            for slot in range(PROMPTS):
                k = place - slot
                far[:, slot * tokens : (slot + 1) * tokens] = (
                    moved[k - 1][...] if k > 0 else own[...]
                )

    head = HEAD_DIM
    block = tokens // 2
    key_far, value_far = far[:head].T, far[head:]
    key_own = own[:head].T
    total = far.shape[1]
    near_row = lax.broadcasted_iota(jnp.int32, (block, block), 0)
    near_col = lax.broadcasted_iota(jnp.int32, (block, block), 1)
    causal = near_row <= near_col
    row = lax.broadcasted_iota(jnp.int32, (total, block), 0)
    for part in range(2):
        cols = slice(part * block, (part + 1) * block)
        key_near, value_near = key_own[cols], own[head:, cols]
        seen = row < table[COUNT + part] * block

        def one(h, _):
            at = pl.ds(pl.multiple_of(h * head, head), head)
            rows = query[at, cols]
            score_far = jnp.where(seen, dims(key_far, rows, 1, 0) * score_scale, neg_big)
            score_near = jnp.where(causal, dims(key_near, rows, 1, 0) * score_scale, neg_big)
            top = jnp.maximum(
                jnp.max(score_far, axis=0, keepdims=True), jnp.max(score_near, axis=0, keepdims=True)
            )
            weight_far = jnp.exp(score_far - top)
            weight_near = jnp.exp(score_near - top)
            weight = jnp.sum(weight_far, axis=0, keepdims=True) + jnp.sum(
                weight_near, axis=0, keepdims=True
            )
            out = dims(value_far, weight_far.astype(bf16), 1, 0) + dims(
                value_near, weight_near.astype(bf16), 1, 0
            )
            attended[at, cols] = out / weight
            log_total[h, :, cols] = top + jnp.log(weight)
            return 0

        lax.fori_loop(0, query.shape[0] // head, one, 0)
    values = attended[...]
    attended_low[...] = values.astype(bf16)
    flipped = values.T.astype(bf16)
    model = weights.shape[2]
    keep_and_send(
        table,
        lambda b: dims(flipped, weights[b, model:], 1, 0),
        keep_first,
        keep_second,
        send,
    )


def hidden_body(
    table, raw, own_first, own_second, other_first, other_second, gain, hidden, normed, inverse
):
    core = table[C]
    summed, other = (own_first, own_second), (other_first, other_second)
    for i in range(2):
        b = 2 * i + core
        hidden[b] = raw[b].astype(f32) + summed[i][...].astype(f32)
        b = 2 * i + 1 - core
        hidden[b] = raw[b].astype(f32) + other[i][...].astype(f32)

    def square(b, total):
        values = hidden[b]
        return total + jnp.sum(values * values, axis=1, keepdims=True)

    count = raw.shape[0]
    total = lax.fori_loop(0, count, square, jnp.zeros((raw.shape[1], 1), f32))
    scale = lax.rsqrt(total / (count * raw.shape[2]) + eps)
    inverse[...] = scale

    def norm(b, _):
        normed[b] = (hidden[b] * scale * gain[b]).astype(bf16)
        return 0

    lax.fori_loop(0, count, norm, 0)


def gate_body(table, normed, pieces, active, gate_slope, up_slope, weights, acc, sems):
    start_pieces(table, pieces, weights, sems)()
    acc[...] = jnp.zeros_like(acc)

    def one(b, _):
        acc[...] += dims(normed[b], weights[b], 1, 0)
        return 0

    lax.fori_loop(0, normed.shape[0], one, 0)
    half = acc.shape[1] // 2
    rows = acc.shape[0] // 4

    def part(i, _):
        at = pl.ds(pl.multiple_of(i * rows, rows), rows)
        gate, up = acc[at, :half], acc[at, half:]
        sigmoid = jax.nn.sigmoid(gate)
        active[at] = (gate * sigmoid * up).astype(bf16)
        gate_slope[at] = up * sigmoid * (1.0 + gate * (1.0 - sigmoid))
        up_slope[at] = gate * sigmoid
        return 0

    lax.fori_loop(0, 4, part, 0)


def down_parts_body(table, active, grad, *parts):
    flipped = active[...].T
    for k, part in enumerate(parts):
        part[...] = dims(flipped, grad[table[ORDER + k]], 1, 0).astype(bf16)


def gate_back_body(
    table,
    grad,
    gate_slope,
    up_slope,
    gate_pieces,
    down_pieces,
    change,
    keep_first,
    keep_second,
    send,
    gate_weights,
    down_weights,
    acc,
    gate_sems,
    down_sems,
):
    down_wait = start_pieces(table, down_pieces, down_weights, down_sems)
    gate_wait = start_pieces(table, gate_pieces, gate_weights, gate_sems)
    down_wait()
    acc[...] = jnp.zeros_like(acc)

    def one(b, _):
        acc[...] += dims(grad[b], down_weights[b], 1, 1)
        return 0

    lax.fori_loop(0, grad.shape[0], one, 0)
    half = acc.shape[1]
    change[:, :half] = (acc[...] * gate_slope[...]).astype(bf16)
    change[:, half:] = (acc[...] * up_slope[...]).astype(bf16)
    gate_wait()
    values = change[...]
    keep_and_send(
        table, lambda b: dims(values, gate_weights[b], 1, 1), keep_first, keep_second, send
    )


def down_body(table, active, pieces, keep_first, keep_second, send, weights, sems):
    start_pieces(table, pieces, weights, sems)()
    values = active[...]
    keep_and_send(table, lambda b: dims(values, weights[b], 1, 0), keep_first, keep_second, send)


def gate_parts_body(table, normed, change, *parts):
    for k, part in enumerate(parts):
        part[...] = dims(normed[table[ORDER + k]], change[...], 0, 0).astype(bf16)


def attend_back_body(
    table,
    hidden,
    inverse,
    own_first,
    own_second,
    other_first,
    other_second,
    grad,
    gain,
    weights,
    query,
    own,
    far,
    attended,
    log_total,
    cosine,
    sine,
    through,
    pull,
    query_low,
    own_back,
    *rest,
):
    sends, far_back, change = rest[: GROUP - 1], rest[-2], rest[-1]
    core = table[C]
    count, tokens, model = hidden.shape
    for i, (mine, theirs) in enumerate(((own_first, other_first), (own_second, other_second))):
        change[2 * i + core] = mine[...].astype(f32) * gain[2 * i + core]
        change[2 * i + 1 - core] = theirs[...].astype(f32) * gain[2 * i + 1 - core]

    def product(b, total):
        return total + jnp.sum(change[b] * hidden[b], axis=1, keepdims=True)

    inner = lax.fori_loop(0, count, product, jnp.zeros((tokens, 1), f32))
    scale = inverse[...]
    back = scale * scale * scale * inner / (count * model)
    pull[...] = back

    def rows(b, total):
        values = grad[b].astype(f32) + scale * change[b] - hidden[b] * back
        low = values.astype(bf16)
        through[b] = low
        return total + dims(low, weights[b, model:], 1, 1)

    heads_cols = query.shape[0]
    branch = lax.fori_loop(0, count, rows, jnp.zeros((tokens, heads_cols), f32))
    branch = branch.T.astype(bf16)

    head = HEAD_DIM
    block = tokens // 2
    key_far_t = far[:head]
    key_far, value_far = key_far_t.T, far[head:].T
    key_own, value_own = own[:head].T, own[head:].T
    total = far.shape[1]
    near_row = lax.broadcasted_iota(jnp.int32, (block, block), 0)
    near_col = lax.broadcasted_iota(jnp.int32, (block, block), 1)
    causal = near_row <= near_col
    row = lax.broadcasted_iota(jnp.int32, (total, block), 0)
    far_back[...] = jnp.zeros_like(far_back)
    own_back[...] = jnp.zeros_like(own_back)
    for part in range(2):
        cols = slice(part * block, (part + 1) * block)
        key_near, value_near = key_own[cols], value_own[cols]
        key_near_t = own[:head, cols]
        seen = row < table[COUNT + part] * block
        for h in range(heads_cols // head):
            at = slice(h * head, (h + 1) * head)
            rows_q, rows_grad = query[at, cols], branch[at, cols]
            delta = jnp.sum(
                rows_grad.astype(f32) * attended[at, cols], axis=0, keepdims=True
            )
            logs = log_total[h, :, cols]

            def one(key, value, allowed):
                score = dims(key, rows_q, 1, 0) * score_scale
                prob = jnp.where(allowed, jnp.exp(score - logs), 0.0)
                moved = (prob * (dims(value, rows_grad, 1, 0) - delta)).astype(bf16)
                return prob.astype(bf16), moved

            prob_far, moved_far = one(key_far, value_far, seen)
            prob_near, moved_near = one(key_near, value_near, causal)
            query_back = (
                dims(key_far_t, moved_far, 1, 0) + dims(key_near_t, moved_near, 1, 0)
            ) * score_scale
            query_low[at, cols] = turn(query_back, cosine[:, cols], -sine[:, cols]).astype(bf16)
            far_back[:head] += dims(rows_q, moved_far, 1, 1) * score_scale
            far_back[head:] += dims(rows_grad, prob_far, 1, 1)
            own_back[:head, cols] += dims(rows_q, moved_near, 1, 1) * score_scale
            own_back[head:, cols] += dims(rows_grad, prob_near, 1, 1)
    for slot in range(PROMPTS):

        @pl.when(table[Z_IN] == slot)
        def _():
            own_back[...] += far_back[:, slot * tokens : (slot + 1) * tokens]

    for k in range(1, GROUP):
        sends[k - 1][...] = far_back[:, :tokens].astype(bf16)
        for slot in range(1, PROMPTS):

            @pl.when(table[Z_IN] == slot + k)
            def _():
                sends[k - 1][...] = far_back[:, slot * tokens : (slot + 1) * tokens].astype(bf16)


def query_parts_body(table, query_low, normed, attended_low, through, *parts):
    rows = query_low.shape[0]
    for k, part in enumerate(parts):
        b = table[ORDER + k]
        part[:rows] = dims(query_low[...], normed[b], 1, 0).astype(bf16)
        part[rows:] = dims(attended_low[...], through[b], 1, 0).astype(bf16)


def qkv_back_body(table, own_back, *refs):
    moved, refs = refs[: GROUP - 1], refs[GROUP - 1 :]
    query_low, normed, weights, cosine, sine = refs[:5]
    parts, (keep_first, keep_second, send) = refs[5:-3], refs[-3:]
    head = HEAD_DIM
    total = own_back[...]
    for part in moved:
        total = total + part[...].astype(f32)
    key = turn(total[:head], cosine[...], -sine[...])
    low = jnp.concatenate([key, total[head:]], axis=0)
    low_16 = low.astype(bf16)
    for k, part in enumerate(parts):
        part[...] = dims(low_16, normed[table[ORDER + k]], 1, 0).astype(bf16)
    flipped = jnp.concatenate([query_low[...].T, low.T.astype(bf16)], axis=1)
    model = weights.shape[2]
    keep_and_send(
        table,
        lambda b: dims(flipped, weights[b, :model], 1, 1),
        keep_first,
        keep_second,
        send,
    )


def rope_tables(positions, half):
    freq = rope_base ** (-(2.0 * jnp.arange(half, dtype=f32)) / (2.0 * half))
    angle = freq[:, None] * positions.astype(f32)[None, :]
    return (jnp.cos(angle), jnp.sin(angle))


def shards(
    layer_in,
    first_gain,
    query_weight,
    key_matrix,
    value_matrix,
    out_weight,
    second_gain,
    gate_weight,
    up_weight,
    down_weight,
    out_grad,
):
    place = Place()
    n, ny, y, z_in, table = place.n, place.ny, place.y, place.z_in, place.table
    lined = place.lined
    block, width = layer_in.shape
    tokens = 2 * block
    model_width = width * ny
    hidden_dev = gate_weight.shape[1] // 2
    query_rows = query_weight.shape[1] // 2
    kv_rows = key_matrix.shape[1]
    qkv_cols = query_rows + kv_rows
    full = (ny, tokens, width)
    wide = [(full[1:], f32), (full[1:], f32), ((2,) + full[1:], bf16)]

    def by_columns(*matrices):
        mine, other = zip(*(part_of(y, m, 1) for m in matrices))
        got = place.swap_y(jnp.concatenate(other, axis=1))
        return jnp.concatenate(pair(y, jnp.concatenate(mine, axis=1), got), axis=0)

    def by_rows(matrix):
        mine, other = part_of(y, matrix, 0)
        return jnp.concatenate(pair(y, mine, place.swap_y(other)), axis=1)

    def gathered(piece, rows_first):
        if lined:
            return gather_pieces(place, piece)
        return [gather_whole(place, piece, rows_first)]

    qkv_piece = by_columns(query_weight, key_matrix, value_matrix)
    out_piece = by_rows(out_weight)
    if lined:
        attend_pieces = gather_pieces(place, jnp.concatenate([qkv_piece, out_piece], axis=0))
    else:
        attend_pieces = [
            jnp.concatenate(
                [gather_whole(place, qkv_piece, True), gather_whole(place, out_piece, False)],
                axis=1,
            )
        ]
    gate_piece = by_columns(gate_weight, up_weight)
    down_piece = by_rows(down_weight)
    gate_pieces = gathered(after(gate_piece, attend_pieces[len(attend_pieces) // 2]), True)
    down_pieces = gathered(after(down_piece, gate_pieces[len(gate_pieces) // 2]), False)
    attend_shape = (ny, width + query_rows, width)
    gate_shape = (ny, width, 2 * hidden_dev)
    down_shape = (ny, hidden_dev, width)
    sems = pltpu.SemaphoreType.DMA((ny,))

    def spread(value):
        by_x = place.swap_x(value)
        four = [value, by_x, place.swap_y(value), place.swap_y(by_x)]
        return four + [place.swap_c(r) for r in four]

    gains = jnp.stack([first_gain, second_gain])
    two = [gains, place.swap_x(gains)]
    gains = two + [place.swap_c(g) for g in two]
    raw, normed_in, inverse_in, gain_in, gain_mid = call(
        rows_body,
        [(full, bf16), (full, bf16), ((tokens, 1), f32)] + [((ny, 1, width), f32)] * 2,
        table,
        spread(layer_in) + gains,
        earlier=[gate_piece, down_piece],
    )

    within = jnp.arange(block, dtype=jnp.int32)
    positions = jnp.minimum(place.offset, PROMPT_DEV)[:, None] * block + within[None, :]
    cosine, sine = rope_tables(positions.reshape(-1), HEAD_DIM // 2)
    query, own, attend_weights = call(
        qkv_body,
        [((query_rows, tokens), bf16), ((kv_rows, tokens), bf16), (attend_shape, bf16)],
        table,
        [normed_in, cosine, sine],
        [attend_pieces],
        [pltpu.VMEM((tokens, qkv_cols), f32), sems],
    )
    moved = [
        place.send_z(
            own,
            [(s, s + k) for s in range(n) if s % GROUP < PROMPTS and s % GROUP + k < GROUP],
        )
        for k in range(1, GROUP)
    ]
    (grad,) = call(grad_body, [(full, bf16)], table, spread(after(out_grad, normed_in)))
    attended, attended_low, log_total, far, keep_first, keep_second, send = call(
        attend_body,
        [
            ((query_rows, tokens), f32),
            ((query_rows, tokens), bf16),
            ((query_rows // HEAD_DIM, 1, tokens), f32),
            ((kv_rows, PROMPTS * tokens), bf16),
        ]
        + wide,
        table,
        [query, own] + moved + [attend_weights],
        earlier=[grad, gate_pieces[len(gate_pieces) // 4]],
    )
    summed = all_sum(place, (keep_first, keep_second), send, gate_pieces[len(gate_pieces) // 2])

    hidden, normed_mid, inverse_mid = call(
        hidden_body,
        [(full, f32), (full, bf16), ((tokens, 1), f32)],
        table,
        [raw] + summed + [gain_mid],
        earlier=[gate_pieces[-1], down_pieces[len(down_pieces) // 4]],
    )
    active, gate_slope, up_slope = call(
        gate_body,
        [((tokens, hidden_dev), bf16)] + [((tokens, hidden_dev), f32)] * 2,
        table,
        [normed_mid],
        [gate_pieces],
        [
            pltpu.VMEM(gate_shape, bf16),
            pltpu.VMEM((tokens, 2 * hidden_dev), f32),
            sems,
        ],
        earlier=[down_pieces[len(down_pieces) // 2]],
    )
    down_parts = call(down_parts_body, [(down_shape[1:], bf16)] * ny, table, [active, grad])
    change, keep_first, keep_second, send = call(
        gate_back_body,
        [((tokens, 2 * hidden_dev), bf16)] + wide,
        table,
        [grad, gate_slope, up_slope],
        [gate_pieces, down_pieces],
        [
            pltpu.VMEM(gate_shape, bf16),
            pltpu.VMEM(down_shape, bf16),
            pltpu.VMEM((tokens, hidden_dev), f32),
            sems,
            sems,
        ],
        earlier=[down_parts[0]],
    )
    summed = all_sum(place, (keep_first, keep_second), send)
    keep_first, keep_second, send = call(
        down_body,
        wide,
        table,
        [active],
        [down_pieces],
        [pltpu.VMEM(down_shape, bf16), sems],
        earlier=[summed[-1]],
    )
    hidden_own = own_block(place, hidden)
    layer_out = (hidden_own + own_sum(place, (keep_first, keep_second), send)).astype(bf16)
    down_grad = scatter_sum(place, down_parts, False)
    gate_parts = call(gate_parts_body, [(gate_shape[1:], bf16)] * ny, table, [normed_mid, change])
    gate_grad = scatter_sum(place, gate_parts, True)

    through, pull, query_low, own_back, *sends = call(
        attend_back_body,
        [
            (full, bf16),
            ((tokens, 1), f32),
            ((query_rows, tokens), bf16),
            ((kv_rows, tokens), f32),
        ]
        + [((kv_rows, tokens), bf16)] * (GROUP - 1),
        table,
        [hidden, inverse_mid]
        + summed
        + [
            grad,
            gain_mid,
            attend_weights,
            query,
            own,
            far,
            attended,
            log_total,
            cosine,
            sine,
        ],
        scratch=[pltpu.VMEM((kv_rows, PROMPTS * tokens), f32), pltpu.VMEM(full, f32)],
    )
    inverse_own, _ = part_of(y, inverse_mid, 0)
    pull_own, _ = part_of(y, pull, 0)
    mid_own = jnp.where(place.x == 0, summed[0], summed[1])
    mid_own = part_of(y, mid_own, 0)[0].astype(f32)
    through_own = (
        out_grad.astype(f32)
        + inverse_own * mid_own * second_gain[None, :]
        - hidden_own * pull_own
    )
    second_term = jnp.sum(mid_own * hidden_own * inverse_own, axis=0)

    query_parts = call(
        query_parts_body,
        [((2 * query_rows, width), bf16)] * ny,
        table,
        [query_low, normed_in, attended_low, through],
    )
    query_grad = scatter_sum(place, query_parts, False)

    moved = [
        place.send_z(
            sends[k - 1],
            [(s, s - k) for s in range(n) if 0 <= s % GROUP - k < PROMPTS],
        )
        for k in range(1, GROUP)
    ]
    *kv_parts, keep_first, keep_second, send = call(
        qkv_back_body,
        [((kv_rows, width), bf16)] * ny + wide,
        table,
        [own_back] + moved + [query_low, normed_in, attend_weights, cosine, sine],
    )
    kv_grad = scatter_sum(place, kv_parts, False)
    first_own = own_sum(place, (keep_first, keep_second), send)
    input_own = layer_in.astype(f32)
    inverse_own, _ = part_of(y, inverse_in, 0)
    scaled = first_own * first_gain[None, :]
    inner = jnp.sum(scaled * input_own, axis=1, keepdims=True)
    inner = inner + place.swap_c(inner)
    inner = inner + place.swap_x(inner)
    in_grad = (
        through_own + inverse_own * scaled - input_own * (inverse_own**3 * inner / model_width)
    )
    first_term = jnp.sum(first_own * input_own * inverse_own, axis=0)
    terms = jnp.stack([first_term, second_term])
    bit = 1
    while bit < place.nx:
        terms = terms + place.swap_gx(terms, bit)
        bit *= 2

    def joined(summed_part, axis):
        mine, other = part_of(y, summed_part, axis)
        return pair(y, mine, place.swap_y(other.astype(bf16)).astype(f32))

    gate_low, gate_high = joined(gate_grad, 0)
    down_grad = jnp.concatenate(joined(down_grad, 1), axis=0)
    query_low, query_high = joined(query_grad, 1)
    kv_low, kv_high = joined(kv_grad, 1)

    def stacked(low, high, start, stop):
        return jnp.concatenate([low[start:stop], high[start:stop]], axis=0)

    half_kv = kv_rows // 2
    return (
        layer_out,
        in_grad,
        terms[0],
        stacked(query_low, query_high, 0, query_rows).T,
        stacked(kv_low, kv_high, 0, half_kv).T,
        stacked(kv_low, kv_high, half_kv, kv_rows).T,
        stacked(query_low, query_high, query_rows, 2 * query_rows),
        terms[1],
        jnp.concatenate([gate_low[:, :hidden_dev], gate_high[:, :hidden_dev]], axis=1),
        jnp.concatenate([gate_low[:, hidden_dev:], gate_high[:, hidden_dev:]], axis=1),
        down_grad,
    )


def solution(mesh):
    rows, cols, gain = P("gx", "gy"), P("gy", "gx"), P("gy")
    return jax.shard_map(
        shards,
        mesh=mesh,
        in_specs=(rows, gain, rows, rows, rows, cols, gain, rows, rows, cols, rows),
        out_specs=(rows, rows, gain, rows, rows, rows, cols, gain, rows, rows, cols),
        check_vma=False,
    )
```

profile of v0, /device:TPU:0, one launch (start us, length us, event | category | flops | bytes accessed | tf_op | source)
XLA Modules:
  0.0 458.0 jit_solution(719679633359377273)
XLA Ops:
  11.2 14.7 %collective-permute-done.13 = bf16[192,192]{1,0:T(8,128)(2,1)S(1)} collective-permute-done((bf16[192,192]{1,0:T(8,128)(2,1)S(1)}, bf16[192,192]{1,0:T(8,128)(2,1)S(1)}, u32[]{:S(2)}, u32[]{:S(2)}) %collective-permute-start.13) | collective-permute-done | bytes 73760 | tf_op jit(solution)/shard_map/ppermute | solution.py:49
  27.4 3.9 collective-permute-done.12
  49.5 13.8 %collective-permute-done.15.refs_5_ = bf16[576,384]{1,0:T(8,128)(2,1)S(1)} collective-permute-done((bf16[576,384]{1,0:T(8,128)(2,1)S(1)}, bf16[576,384]{1,0:T(8,128)(2,1)S(1)}, u32[]{:S(2)}, u32[]{:S(2)}) %collective-permute-start.15) | collective-permute-done | bytes 442400 | tf_op jit(solution)/shard_map/ppermute | solution.py:62
  66.9 4.3 collective-permute-done.22.refs_2_
  74.3 16.4 %collective-permute-done.17.refs_7_ = bf16[576,384]{1,0:T(8,128)(2,1)S(1)} collective-permute-done((bf16[576,384]{1,0:T(8,128)(2,1)S(1)}, bf16[576,384]{1,0:T(8,128)(2,1)S(1)}, u32[]{:S(2)}, u32[]{:S(2)}) %collective-permute-start.17) | collective-permute-done | bytes 442400 | tf_op jit(solution)/shard_map/ppermute | solution.py:62
  90.8 3.5 shard_map.195
  95.8 4.0 collective-permute-start.19
  105.3 3.9 collective-permute-done.20.refs_4_
  109.2 5.5 %shard_map.197 = (f32[192,512]{1,0:T(8,128)S(1)}, bf16[192,512]{1,0:T(8,128)(2,1)S(1)}, f32[2,1,512]{2,1,0:T(1,128)S(1)}, bf16[192,1024]{1,0:T(8,128)(2,1)S(1)},...) custom-call(s32[11]{0:T(128)S(1)} %concatenate.48.table_ref, ...), custom_call_target="tpu_custom_call" | custom-call | tf_op jit(solution)/shard_map/pallas_call | solution.py:177
  114.8 5.5 %collective-permute-start.32 = (bf16[384,1024]{1,0:T(8,128)(2,1)S(1)}, bf16[384,1024]{1,0:T(8,128)(2,1)S(1)}, u32[]{:S(2)}, u32[]{:S(2)}) collective-permute-start(bf16[384,1024]{1,0:T(8,128)(2,1)S(1)} %pad_maximum_fusion.1.refs_12_.refs_1_.refs_3_), channel_id=1, source_target_pairs={{0,16},{4,20},{8,24},{12,28},{16,0},{20,4},{24,8},{28,12},{1,17},{... | collective-permute-start | bytes 2359304 | tf_op jit(solution)/shard_map/ppermute | solution.py:62
  121.6 10.1 %collective-permute-done.30 = bf16[512,384]{1,0:T(8,128)(2,1)S(1)} collective-permute-done((bf16[512,384]{1,0:T(8,128)(2,1)S(1)}, bf16[512,384]{1,0:T(8,128)(2,1)S(1)}, u32[]{:S(2)}, u32[]{:S(2)}) %collective-permute-start.30) | collective-permute-done | bytes 393248 | tf_op jit(solution)/shard_map/ppermute | solution.py:55
  132.4 22.9 %collective-permute-done.32.refs_3_.refs_5_ = bf16[384,1024]{1,0:T(8,128)(2,1)S(1)} collective-permute-done((bf16[384,1024]{1,0:T(8,128)(2,1)S(1)}, bf16[384,1024]{1,0:T(8,128)(2,1)S(1)}, u32[]{:S(2)}, u32[]{:S(2)}) %collective-permute-start.32) | collective-permute-done | bytes 786464 | tf_op jit(solution)/shard_map/ppermute | solution.py:62
  161.1 5.1 %collective-permute-done.33 = bf16[512,384]{1,0:T(8,128)(2,1)S(1)} collective-permute-done((bf16[512,384]{1,0:T(8,128)(2,1)S(1)}, bf16[512,384]{1,0:T(8,128)(2,1)S(1)}, u32[]{:S(2)}, u32[]{:S(2)}) %collective-permute-start.33) | collective-permute-done | bytes 393248 | tf_op jit(solution)/shard_map/ppermute | solution.py:49
  168.2 16.9 %collective-permute-done.38.refs_7_.refs_9_.refs_2_ = bf16[512,384]{1,0:T(8,128)(2,1)S(1)} collective-permute-done((bf16[512,384]{1,0:T(8,128)(2,1)S(1)}, bf16[512,384]{1,0:T(8,128)(2,1)S(1)}, u32[]{:S(2)}, u32[]{:S(2)}) %collective-permute-start.38) | collective-permute-done | bytes 393248 | tf_op jit(solution)/shard_map/ppermute | solution.py:62
  185.1 13.0 %collective-permute-done.40.refs_6_.refs_10_.refs_3_ = bf16[512,384]{1,0:T(8,128)(2,1)S(1)} collective-permute-done((bf16[512,384]{1,0:T(8,128)(2,1)S(1)}, bf16[512,384]{1,0:T(8,128)(2,1)S(1)}, u32[]{:S(2)}, u32[]{:S(2)}) %collective-permute-start.40) | collective-permute-done | bytes 393248 | tf_op jit(solution)/shard_map/ppermute | solution.py:62
  204.4 4.5 shard_map.199
  211.6 6.6 %shard_map.201 = (bf16[512,1024]{1,0:T(8,128)(2,1)S(1)}, f32[512,384]{1,0:T(8,128)S(1)}, f32[512,384]{1,0:T(8,128)S(1)}, bf16[2,512,384]{2,1,0:T(8,128)(2,1)S(1)}) custom-call(s32[11]{0:T(128)S(1)} %concatenate.48.table_ref, bf16[4,512,384]{2,1,0:T(8,128)(2,1)S(1)} %shard_map.196.refs_6_.refs_1_.refs_0_, f32[512,512]{1,0:T(8,128)S(1)} %get-tuple-element.86.refs_1_, ...), custom_call_target="tpu_custom_call" | custom-call | tf_op jit(solution)/shard_map/pallas_call | solution.py:177
  224.2 5.4 %collective-permute-start.76 = (bf16[384,1024]{1,0:T(8,128)(2,1)}, bf16[384,1024]{1,0:T(8,128)(2,1)}, u32[]{:S(2)}, u32[]{:S(2)}) collective-permute-start(bf16[384,1024]{1,0:T(8,128)(2,1)} %get-tuple-element.122), channel_id=1, source_target_pairs={{0,8},{4,12},{24,16},{28,20},{1,9},{5,13},{25,17},{29,21},{2,10},{... | collective-permute-start | bytes 2359304 | tf_op jit(solution)/shard_map/ppermute | solution.py:62
  233.1 22.3 %collective-permute-done.81 = bf16[512,384]{1,0:T(8,128)(2,1)S(1)} collective-permute-done((bf16[512,384]{1,0:T(8,128)(2,1)}, bf16[512,384]{1,0:T(8,128)(2,1)S(1)}, u32[]{:S(2)}, u32[]{:S(2)}) %collective-permute-start.81) | collective-permute-done | bytes 393248 | tf_op jit(solution)/shard_map/ppermute | solution.py:62
  256.3 3.6 collective-permute-start.82
  267.6 10.7 %collective-permute-done.82 = bf16[512,384]{1,0:T(8,128)(2,1)} collective-permute-done((bf16[512,384]{1,0:T(8,128)(2,1)}, bf16[512,384]{1,0:T(8,128)(2,1)}, u32[]{:S(2)}, u32[]{:S(2)}) %collective-permute-start.82) | collective-permute-done | bytes 393248 | tf_op jit(solution)/shard_map/ppermute | solution.py:62
  282.2 4.9 %collective-permute-done.83 = bf16[512,192]{1,0:T(8,128)(2,1)S(1)} collective-permute-done((bf16[512,192]{1,0:T(8,128)(2,1)S(1)}, bf16[512,192]{1,0:T(8,128)(2,1)S(1)}, u32[]{:S(2)}, u32[]{:S(2)}) %collective-permute-start.83) | collective-permute-done | bytes 196640 | tf_op jit(solution)/shard_map/ppermute | solution.py:49
  291.3 3.4 collective-permute-done.44
  299.3 23.2 %collective-permute-done.77 = bf16[384,1024]{1,0:T(8,128)(2,1)S(1)} collective-permute-done((bf16[384,1024]{1,0:T(8,128)(2,1)S(1)}, bf16[384,1024]{1,0:T(8,128)(2,1)S(1)}, u32[]{:S(2)}, u32[]{:S(2)}) %collective-permute-start.77) | collective-permute-done | bytes 786464 | tf_op jit(solution)/shard_map/ppermute | solution.py:62
  337.8 8.3 %shard_map.203 = (bf16[4,512,384]{2,1,0:T(8,128)(2,1)S(1)}, f32[512,1]{1,0:T(8,128)S(1)}, bf16[192,512]{1,0:T(8,128)(2,1)S(1)}, f32[192,512]{1,0:T(8,128)S(1)}, ...) custom-call(s32[11]{0:T(128)S(1)} %concatenate.48.table_ref, ...), custom_call_target="tpu_custom_call" | custom-call | tf_op jit(solution)/shard_map/pallas_call | solution.py:177
  350.2 5.6 %collective-permute-done.53.refs_1_ = bf16[192,512]{1,0:T(8,128)(2,1)S(1)} collective-permute-done((bf16[192,512]{1,0:T(8,128)(2,1)S(1)}, bf16[192,512]{1,0:T(8,128)(2,1)S(1)}, u32[]{:S(2)}, u32[]{:S(2)}) %collective-permute-start.53) | collective-permute-done | bytes 196640 | tf_op jit(solution)/shard_map/ppermute | solution.py:62
  355.8 9.6 %collective-permute-done.54.refs_2_ = bf16[192,512]{1,0:T(8,128)(2,1)S(1)} collective-permute-done((bf16[192,512]{1,0:T(8,128)(2,1)S(1)}, bf16[192,512]{1,0:T(8,128)(2,1)S(1)}, u32[]{:S(2)}, u32[]{:S(2)}) %collective-permute-start.54) | collective-permute-done | bytes 196640 | tf_op jit(solution)/shard_map/ppermute | solution.py:62
  382.6 3.9 shard_map.202
  398.9 10.1 %collective-permute-done.67 = bf16[384,384]{1,0:T(8,128)(2,1)} collective-permute-done((bf16[384,384]{1,0:T(8,128)(2,1)}, bf16[384,384]{1,0:T(8,128)(2,1)}, u32[]{:S(2)}, u32[]{:S(2)}) %collective-permute-start.67) | collective-permute-done | bytes 294944 | tf_op jit(solution)/shard_map/ppermute | solution.py:62
  417.0 6.0 %collective-permute-done.57 = bf16[512,384]{1,0:T(8,128)(2,1)S(1)} collective-permute-done((bf16[512,384]{1,0:T(8,128)(2,1)S(1)}, bf16[512,384]{1,0:T(8,128)(2,1)S(1)}, u32[]{:S(2)}, u32[]{:S(2)}) %collective-permute-start.57) | collective-permute-done | bytes 393248 | tf_op jit(solution)/shard_map/ppermute | solution.py:55
  425.7 4.5 collective-permute-done.58
  442.8 5.0 %collective-permute-done.48 = bf16[512,384]{1,0:T(8,128)(2,1)S(1)} collective-permute-done((bf16[512,384]{1,0:T(8,128)(2,1)S(1)}, bf16[512,384]{1,0:T(8,128)(2,1)S(1)}, u32[]{:S(2)}, u32[]{:S(2)}) %collective-permute-start.48) | collective-permute-done | bytes 393248 | tf_op jit(solution)/shard_map/ppermute | solution.py:55
  (378 shorter events, 175.0 us)
Async XLA Ops:
  2.1 29.9 %collective-permute-start.7 = (f32[2,384]{1,0:T(2,128)S(1)}, f32[2,384]{1,0:T(2,128)S(1)}, u32[]{:S(2)}, u32[]{:S(2)}) collective-permute-start(f32[2,384]{1,0:T(2,128)S(1)} %pad_maximum_fusion.10.refs_8_), channel_id=1, source_target_pairs={{0,2},{1,3},{2,0},{3,1},{4,6},{5,7},{6,4},{7,5},{8,10},{9,11},{10,... | collective-permute-start | bytes 9224 | tf_op jit(solution)/shard_map/ppermute | solution.py:55
  5.1 33.5 %collective-permute-start.8 = (f32[2,384]{1,0:T(2,128)S(1)}, f32[2,384]{1,0:T(2,128)S(1)}, u32[]{:S(2)}, u32[]{:S(2)}) collective-permute-start(f32[2,384]{1,0:T(2,128)S(1)} %pad_maximum_fusion.10.refs_8_), channel_id=1, source_target_pairs={{0,1},{1,0},{2,3},{3,2},{4,5},{5,4},{6,7},{7,6},{8,9},{9,8},{10,11... | collective-permute-start | bytes 9224 | tf_op jit(solution)/shard_map/ppermute | solution.py:58
  6.5 27.2 %collective-permute-start.11 = (bf16[512,192]{1,0:T(8,128)(2,1)S(1)}, bf16[512,192]{1,0:T(8,128)(2,1)S(1)}, u32[]{:S(2)}, u32[]{:S(2)}) collective-permute-start(bf16[512,192]{1,0:T(8,128)(2,1)S(1)} %broadcast_select_fusion.5), channel_id=1, source_target_pairs={{0,4},{4,0},{8,12},{12,8},{16,20},{20,16},{24,28},{28,24},{1,5},{5... | collective-permute-start | bytes 589832 | tf_op jit(solution)/shard_map/ppermute | solution.py:49
  8.2 35.8 %collective-permute-start.10 = (bf16[192,1024]{1,0:T(8,128)(2,1)S(1)}, bf16[192,1024]{1,0:T(8,128)(2,1)S(1)}, u32[]{:S(2)}, u32[]{:S(2)}) collective-permute-start(bf16[192,1024]{1,0:T(8,128)(2,1)S(1)} %pad_maximum_fusion.5), channel_id=1, source_target_pairs={{0,4},{4,0},{8,12},{12,8},{16,20},{20,16},{24,28},{28,24},{1,5},{5... | collective-permute-start | bytes 1179656 | tf_op jit(solution)/shard_map/ppermute | solution.py:49
  39.8 23.4 %collective-permute-start.15 = (bf16[576,384]{1,0:T(8,128)(2,1)S(1)}, bf16[576,384]{1,0:T(8,128)(2,1)S(1)}, u32[]{:S(2)}, u32[]{:S(2)}) collective-permute-start(bf16[576,384]{1,0:T(8,128)(2,1)S(1)} %maximum_maximum_fusion.refs_3_), channel_id=1, source_target_pairs={{0,16},{4,20},{8,24},{12,28},{16,0},{20,4},{24,8},{28,12},{1,17},{... | collective-permute-start | bytes 1327112 | tf_op jit(solution)/shard_map/ppermute | solution.py:62
  42.4 21.4 %collective-permute-start.14 = (bf16[576,384]{1,0:T(8,128)(2,1)S(1)}, bf16[576,384]{1,0:T(8,128)(2,1)S(1)}, u32[]{:S(2)}, u32[]{:S(2)}) collective-permute-start(bf16[576,384]{1,0:T(8,128)(2,1)S(1)} %maximum_maximum_fusion.refs_3_), channel_id=1, source_target_pairs={{0,8},{4,12},{8,0},{12,4},{16,24},{20,28},{24,16},{28,20},{1,9},{5... | collective-permute-start | bytes 1327112 | tf_op jit(solution)/shard_map/ppermute | solution.py:62
  48.8 18.0 %collective-permute-start.16 = (bf16[576,384]{1,0:T(8,128)(2,1)S(1)}, bf16[576,384]{1,0:T(8,128)(2,1)S(1)}, u32[]{:S(2)}, u32[]{:S(2)}) collective-permute-start(bf16[576,384]{1,0:T(8,128)(2,1)S(1)} %maximum_maximum_fusion.refs_3_), channel_id=1, source_target_pairs={{8,16},{12,20},{16,8},{20,12},{9,17},{13,21},{17,9},{21,13},{10,18... | collective-permute-start | bytes 1327112 | tf_op jit(solution)/shard_map/ppermute | solution.py:62
  63.2 46.0 %collective-permute-start.28 = (bf16[384,1024]{1,0:T(8,128)(2,1)S(1)}, bf16[384,1024]{1,0:T(8,128)(2,1)S(1)}, u32[]{:S(2)}, u32[]{:S(2)}) collective-permute-start(bf16[384,1024]{1,0:T(8,128)(2,1)S(1)} %pad_maximum_fusion.1.refs_12_.refs_1_.refs_3_), channel_id=1, source_target_pairs={{0,8},{4,12},{8,0},{12,4},{16,24},{20,28},{24,16},{28,20},{1,9},{5... | collective-permute-start | bytes 2359304 | tf_op jit(solution)/shard_map/ppermute | solution.py:62
  63.8 26.9 %collective-permute-start.17 = (bf16[576,384]{1,0:T(8,128)(2,1)S(1)}, bf16[576,384]{1,0:T(8,128)(2,1)S(1)}, u32[]{:S(2)}, u32[]{:S(2)}) collective-permute-start(bf16[576,384]{1,0:T(8,128)(2,1)S(1)} %collective-permute-done.15.refs_5_), channel_id=1, source_target_pairs={{8,0},{12,4},{16,24},{20,28},{9,1},{13,5},{17,25},{21,29},{10,2},{... | collective-permute-start | bytes 1327112 | tf_op jit(solution)/shard_map/ppermute | solution.py:62
  66.8 27.5 %collective-permute-start.24 = (bf16[256,384]{1,0:T(8,128)(2,1)S(1)}, bf16[256,384]{1,0:T(8,128)(2,1)S(1)}, u32[]{:S(2)}, u32[]{:S(2)}) collective-permute-start(bf16[256,384]{1,0:T(8,128)(2,1)S(1)} %copy-done.40), channel_id=1, source_target_pairs={{0,1},{1,0},{2,3},{3,2},{4,5},{5,4},{6,7},{7,6},{8,9},{9,8},{10,11... | collective-permute-start | bytes 589832 | tf_op jit(solution)/shard_map/ppermute | solution.py:58
  71.2 24.7 %collective-permute-start.25 = (bf16[256,384]{1,0:T(8,128)(2,1)S(1)}, bf16[256,384]{1,0:T(8,128)(2,1)S(1)}, u32[]{:S(2)}, u32[]{:S(2)}) collective-permute-start(bf16[256,384]{1,0:T(8,128)(2,1)S(1)} %collective-permute-done.21.refs_1_), channel_id=1, source_target_pairs={{0,1},{1,0},{2,3},{3,2},{4,5},{5,4},{6,7},{7,6},{8,9},{9,8},{10,11... | collective-permute-start | bytes 589832 | tf_op jit(solution)/shard_map/ppermute | solution.py:58
  73.9 25.9 %collective-permute-start.26 = (bf16[256,384]{1,0:T(8,128)(2,1)S(1)}, bf16[256,384]{1,0:T(8,128)(2,1)S(1)}, u32[]{:S(2)}, u32[]{:S(2)}) collective-permute-start(bf16[256,384]{1,0:T(8,128)(2,1)S(1)} %collective-permute-done.22.refs_2_), channel_id=1, source_target_pairs={{0,1},{1,0},{2,3},{3,2},{4,5},{5,4},{6,7},{7,6},{8,9},{9,8},{10,11... | collective-permute-start | bytes 589832 | tf_op jit(solution)/shard_map/ppermute | solution.py:58
  114.8 40.4 %collective-permute-start.32 = (bf16[384,1024]{1,0:T(8,128)(2,1)S(1)}, bf16[384,1024]{1,0:T(8,128)(2,1)S(1)}, u32[]{:S(2)}, u32[]{:S(2)}) collective-permute-start(bf16[384,1024]{1,0:T(8,128)(2,1)S(1)} %pad_maximum_fusion.1.refs_12_.refs_1_.refs_3_), channel_id=1, source_target_pairs={{0,16},{4,20},{8,24},{12,28},{16,0},{20,4},{24,8},{28,12},{1,17},{... | collective-permute-start | bytes 2359304 | tf_op jit(solution)/shard_map/ppermute | solution.py:62
  155.8 43.0 %collective-permute-start.37 = (bf16[384,1024]{1,0:T(8,128)(2,1)S(1)}, bf16[384,1024]{1,0:T(8,128)(2,1)S(1)}, u32[]{:S(2)}, u32[]{:S(2)}) collective-permute-start(bf16[384,1024]{1,0:T(8,128)(2,1)S(1)} %collective-permute-done.32.refs_3_.refs_5_), channel_id=1, source_target_pairs={{8,0},{12,4},{16,24},{20,28},{9,1},{13,5},{17,25},{21,29},{10,2},{... | collective-permute-start | bytes 2359304 | tf_op jit(solution)/shard_map/ppermute | solution.py:62
  157.7 27.4 %collective-permute-start.38 = (bf16[512,384]{1,0:T(8,128)(2,1)S(1)}, bf16[512,384]{1,0:T(8,128)(2,1)S(1)}, u32[]{:S(2)}, u32[]{:S(2)}) collective-permute-start(bf16[512,384]{1,0:T(8,128)(2,1)S(1)} %pad_maximum_fusion.6.refs_13_.refs_8_.refs_1_), channel_id=1, source_target_pairs={{0,8},{4,12},{8,0},{12,4},{16,24},{20,28},{24,16},{28,20},{1,9},{5... | collective-permute-start | bytes 1179656 | tf_op jit(solution)/shard_map/ppermute | solution.py:62
  160.3 44.0 %collective-permute-start.39 = (bf16[384,1024]{1,0:T(8,128)(2,1)S(1)}, bf16[384,1024]{1,0:T(8,128)(2,1)S(1)}, u32[]{:S(2)}, u32[]{:S(2)}) collective-permute-start(bf16[384,1024]{1,0:T(8,128)(2,1)S(1)} %pad_maximum_fusion.1.refs_12_.refs_1_.refs_3_), channel_id=1, source_target_pairs={{8,16},{12,20},{16,8},{20,12},{9,17},{13,21},{17,9},{21,13},{10,18... | collective-permute-start | bytes 2359304 | tf_op jit(solution)/shard_map/ppermute | solution.py:62
  166.1 32.0 %collective-permute-start.40 = (bf16[512,384]{1,0:T(8,128)(2,1)S(1)}, bf16[512,384]{1,0:T(8,128)(2,1)S(1)}, u32[]{:S(2)}, u32[]{:S(2)}) collective-permute-start(bf16[512,384]{1,0:T(8,128)(2,1)S(1)} %pad_maximum_fusion.6.refs_13_.refs_8_.refs_1_), channel_id=1, source_target_pairs={{0,16},{4,20},{8,24},{12,28},{16,0},{20,4},{24,8},{28,12},{1,17},{... | collective-permute-start | bytes 1179656 | tf_op jit(solution)/shard_map/ppermute | solution.py:62
  168.1 32.0 %collective-permute-start.35 = (bf16[512,384]{1,0:T(8,128)(2,1)S(1)}, bf16[512,384]{1,0:T(8,128)(2,1)S(1)}, u32[]{:S(2)}, u32[]{:S(2)}) collective-permute-start(bf16[512,384]{1,0:T(8,128)(2,1)S(1)} %get-tuple-element.185.refs_1_), channel_id=1, source_target_pairs={{0,1},{1,0},{2,3},{3,2},{4,5},{5,4},{6,7},{7,6},{8,9},{9,8},{10,11... | collective-permute-start | bytes 1179656 | tf_op jit(solution)/shard_map/ppermute | solution.py:58
  224.2 36.6 %collective-permute-start.76 = (bf16[384,1024]{1,0:T(8,128)(2,1)}, bf16[384,1024]{1,0:T(8,128)(2,1)}, u32[]{:S(2)}, u32[]{:S(2)}) collective-permute-start(bf16[384,1024]{1,0:T(8,128)(2,1)} %get-tuple-element.122), channel_id=1, source_target_pairs={{0,8},{4,12},{24,16},{28,20},{1,9},{5,13},{25,17},{29,21},{2,10},{... | collective-permute-start | bytes 2359304 | tf_op jit(solution)/shard_map/ppermute | solution.py:62
  229.6 25.8 %collective-permute-start.81 = (bf16[512,384]{1,0:T(8,128)(2,1)}, bf16[512,384]{1,0:T(8,128)(2,1)S(1)}, u32[]{:S(2)}, u32[]{:S(2)}) collective-permute-start(bf16[512,384]{1,0:T(8,128)(2,1)} %get-tuple-element.125), channel_id=1, source_target_pairs={{0,8},{4,12},{24,16},{28,20},{1,9},{5,13},{25,17},{29,21},{2,10},{... | collective-permute-start | bytes 1179656 | tf_op jit(solution)/shard_map/ppermute | solution.py:62
  230.9 35.4 %collective-permute-start.80 = (bf16[512,384]{1,0:T(8,128)(2,1)}, bf16[512,384]{1,0:T(8,128)(2,1)}, u32[]{:S(2)}, u32[]{:S(2)}) collective-permute-start(bf16[512,384]{1,0:T(8,128)(2,1)} %get-tuple-element.125), channel_id=1, source_target_pairs={{8,16},{12,20},{16,8},{20,12},{9,17},{13,21},{17,9},{21,13},{10,18... | collective-permute-start | bytes 1179656 | tf_op jit(solution)/shard_map/ppermute | solution.py:62
  232.4 31.5 %collective-permute-start.79 = (bf16[512,384]{1,0:T(8,128)(2,1)}, bf16[512,384]{1,0:T(8,128)(2,1)}, u32[]{:S(2)}, u32[]{:S(2)}) collective-permute-start(bf16[512,384]{1,0:T(8,128)(2,1)} %get-tuple-element.124), channel_id=1, source_target_pairs={{0,8},{4,12},{8,0},{12,4},{16,24},{20,28},{24,16},{28,20},{1,9},{5... | collective-permute-start | bytes 1179656 | tf_op jit(solution)/shard_map/ppermute | solution.py:62
  256.3 22.0 %collective-permute-start.82 = (bf16[512,384]{1,0:T(8,128)(2,1)}, bf16[512,384]{1,0:T(8,128)(2,1)}, u32[]{:S(2)}, u32[]{:S(2)}) collective-permute-start(bf16[512,384]{1,0:T(8,128)(2,1)} %add_convert_fusion.1), channel_id=1, source_target_pairs={{0,16},{4,20},{8,24},{12,28},{16,0},{20,4},{24,8},{28,12},{1,17},{... | collective-permute-start | bytes 1179656 | tf_op jit(solution)/shard_map/ppermute | solution.py:62
  259.9 39.4 %collective-permute-start.75 = (bf16[384,1024]{1,0:T(8,128)(2,1)}, bf16[384,1024]{1,0:T(8,128)(2,1)S(1)}, u32[]{:S(2)}, u32[]{:S(2)}) collective-permute-start(bf16[384,1024]{1,0:T(8,128)(2,1)} %get-tuple-element.122), channel_id=1, source_target_pairs={{8,16},{12,20},{16,8},{20,12},{9,17},{13,21},{17,9},{21,13},{10,18... | collective-permute-start | bytes 2359304 | tf_op jit(solution)/shard_map/ppermute | solution.py:62
  260.8 20.7 %collective-permute-start.43 = (bf16[2,512,384]{2,1,0:T(8,128)(2,1)}, bf16[2,512,384]{2,1,0:T(8,128)(2,1)S(1)}, u32[]{:S(2)}, u32[]{:S(2)}) collective-permute-start(bf16[2,512,384]{2,1,0:T(8,128)(2,1)} %copy-done.55), channel_id=1, source_target_pairs={{0,1},{1,0},{2,3},{3,2},{4,5},{5,4},{6,7},{7,6},{8,9},{9,8},{10,11... | collective-permute-start | bytes 2359304 | tf_op jit(solution)/shard_map/ppermute | solution.py:58
  263.9 35.4 %collective-permute-start.74 = (bf16[384,1024]{1,0:T(8,128)(2,1)S(1)}, bf16[384,1024]{1,0:T(8,128)(2,1)S(1)}, u32[]{:S(2)}, u32[]{:S(2)}) collective-permute-start(bf16[384,1024]{1,0:T(8,128)(2,1)S(1)} %copy-done.54), channel_id=1, source_target_pairs={{0,8},{4,12},{8,0},{12,4},{16,24},{20,28},{24,16},{28,20},{1,9},{5... | collective-permute-start | bytes 2359304 | tf_op jit(solution)/shard_map/ppermute | solution.py:62
  266.4 56.1 %collective-permute-start.77 = (bf16[384,1024]{1,0:T(8,128)(2,1)S(1)}, bf16[384,1024]{1,0:T(8,128)(2,1)S(1)}, u32[]{:S(2)}, u32[]{:S(2)}) collective-permute-start(bf16[384,1024]{1,0:T(8,128)(2,1)S(1)} %add_convert_fusion), channel_id=1, source_target_pairs={{0,16},{4,20},{8,24},{12,28},{16,0},{20,4},{24,8},{28,12},{1,17},{... | collective-permute-start | bytes 2359304 | tf_op jit(solution)/shard_map/ppermute | solution.py:62
  295.7 29.8 %collective-permute-start.45 = (bf16[512,384]{1,0:T(8,128)(2,1)S(1)}, bf16[512,384]{1,0:T(8,128)(2,1)S(1)}, u32[]{:S(2)}, u32[]{:S(2)}) collective-permute-start(bf16[512,384]{1,0:T(8,128)(2,1)S(1)} %get-tuple-element.180), channel_id=1, source_target_pairs={{0,2},{1,3},{2,0},{3,1},{4,6},{5,7},{6,4},{7,5},{8,10},{9,11},{10,... | collective-permute-start | bytes 1179656 | tf_op jit(solution)/shard_map/ppermute | solution.py:55
  297.8 27.7 %collective-permute-start.51 = (bf16[512,384]{1,0:T(8,128)(2,1)S(1)}, bf16[512,384]{1,0:T(8,128)(2,1)S(1)}, u32[]{:S(2)}, u32[]{:S(2)}) collective-permute-start(bf16[512,384]{1,0:T(8,128)(2,1)S(1)} %get-tuple-element.181), channel_id=1, source_target_pairs={{0,4},{4,0},{8,12},{12,8},{16,20},{20,16},{24,28},{28,24},{1,5},{5... | collective-permute-start | bytes 1179656 | tf_op jit(solution)/shard_map/ppermute | solution.py:49
  347.5 17.9 %collective-permute-start.54 = (bf16[192,512]{1,0:T(8,128)(2,1)S(1)}, bf16[192,512]{1,0:T(8,128)(2,1)S(1)}, u32[]{:S(2)}, u32[]{:S(2)}) collective-permute-start(bf16[192,512]{1,0:T(8,128)(2,1)S(1)} %get-tuple-element.103), channel_id=1, source_target_pairs={{16,0},{20,4},{24,8},{28,12},{17,1},{21,5},{25,9},{29,13},{18,2},{... | collective-permute-start | bytes 589832 | tf_op jit(solution)/shard_map/ppermute | solution.py:62
  387.7 47.3 %collective-permute-start.47 = (bf16[2,512,384]{2,1,0:T(8,128)(2,1)}, bf16[2,512,384]{2,1,0:T(8,128)(2,1)}, u32[]{:S(2)}, u32[]{:S(2)}) collective-permute-start(bf16[2,512,384]{2,1,0:T(8,128)(2,1)} %get-tuple-element.92), channel_id=1, source_target_pairs={{0,1},{1,0},{2,3},{3,2},{4,5},{5,4},{6,7},{7,6},{8,9},{9,8},{10,11... | collective-permute-start | bytes 2359304 | tf_op jit(solution)/shard_map/ppermute | solution.py:58
  387.7 23.8 %collective-permute-start.56 = (bf16[2,512,384]{2,1,0:T(8,128)(2,1)}, bf16[2,512,384]{2,1,0:T(8,128)(2,1)}, u32[]{:S(2)}, u32[]{:S(2)}) collective-permute-start(bf16[2,512,384]{2,1,0:T(8,128)(2,1)} %get-tuple-element.107), channel_id=1, source_target_pairs={{0,1},{1,0},{2,3},{3,2},{4,5},{5,4},{6,7},{7,6},{8,9},{9,8},{10,11... | collective-permute-start | bytes 2359304 | tf_op jit(solution)/shard_map/ppermute | solution.py:58
  (120 other events, 1318.8 us)
where the time goes:
time: 459 us; the launch traced here: 458 us
  waiting for transfers between devices  259 us (56%)
  starting transfers between devices  97.6 us (21%)
  Pallas kernels  48.4 us (11%)
  other arithmetic  30.9 us (7%)
  local copies, waits for them, and re-layouts  20.3 us (4%)
    ppermute x34, waiting for transfers between devices, send_z(): return lax.ppermute(value, 'gx', pairs)  172 us
    ppermute x34, starting transfers between devices, send_z(): return lax.ppermute(value, 'gx', pairs)  59.3 us
    ppermute x21, waiting for transfers between devices, swap_gx(): return lax.ppermute(value, 'gx', [(i, i ^ bit) for i in range(self.nx)])  55.3 us
    pallas_call x13, Pallas kernels, call(): pl.pallas_call(kernel, out_shape=[jax.ShapeDtypeStruct(shape, dtype) for...  48.4 us
    ppermute x10, waiting for transfers between devices, swap_x(): return lax.ppermute(value, 'gy', [(i, i ^ 2) for i in range(self.ny)])  29.2 us
    ppermute x21, starting transfers between devices, swap_gx(): return lax.ppermute(value, 'gx', [(i, i ^ bit) for i in range(self.nx)])  22.8 us
    unnamed x146, local copies, waits for them, and re-layouts  15.4 us
    ppermute x10, starting transfers between devices, swap_x(): return lax.ppermute(value, 'gy', [(i, i ^ 2) for i in range(self.ny)])  13.5 us
  transfers between devices with their start and end apart: 84, of which 39 were waited for; matrix products, arithmetic and copies ran while one was open for 9% of the time, Pallas kernels for 5%

commit v1 on v0

--- a/solution.py
+++ b/solution.py
@@ -1,3 +1,5 @@
+from functools import partial
+
 import jax
 import jax.numpy as jnp
 from jax import lax
@@ -92,28 +94,28 @@
     return [piece, near, second, middle, place.send_z(second, OUTWARD)]
 
 
-def gather_whole(place, piece, by_rows):
+def gather_whole(place, piece):
     every = lax.all_gather(piece, "gx", axis_index_groups=place.by_y())
     inner = place.n // place.ny
+    if inner == 1:
+        return every
     rows, cols = piece.shape
-    if by_rows:
-        return every.reshape(place.ny, inner * rows, cols)
     every = every.reshape(place.ny, inner, rows, cols)
     return jnp.swapaxes(every, 1, 2).reshape(place.ny, rows, inner * cols)
 
 
-def scatter_sum(place, parts, by_rows):
+def scatter_whole(place, parts):
+    inner = place.n // place.ny
+    if inner > 1:
+        count, rows, cols = parts.shape
+        parts = jnp.swapaxes(parts.reshape(count, rows, inner, cols // inner), 1, 2)
+        parts = parts.reshape(place.n, rows, cols // inner)
+    return lax.psum_scatter(parts, "gx", axis_index_groups=place.by_y())
+
+
+def scatter_sum(place, parts):
     if not place.lined:
-        n = place.n
-        inner = n // place.ny
-        parts = jnp.stack(parts)
-        count, rows, cols = parts.shape
-        if by_rows:
-            parts = parts.reshape(n, rows // inner, cols)
-        else:
-            parts = jnp.swapaxes(parts.reshape(count, rows, inner, cols // inner), 1, 2)
-            parts = parts.reshape(n, rows, cols // inner)
-        return lax.psum_scatter(parts, "gx", axis_index_groups=place.by_y()).astype(f32)
+        return scatter_whole(place, jnp.stack(parts)).astype(f32)
     own, near, second, third = parts
     far = place.send_z(third, INWARD)
     near = place.send_z(near, NEAR)
@@ -122,15 +124,13 @@
     return own.astype(f32) + near.astype(f32) + middle.astype(f32) + second.astype(f32)
 
 
-def all_sum(place, keep, send, *earlier):
+def all_sum(place, keep, send):
     got = place.swap_c(send)
     first, second = keep[0] + got[0].astype(f32), keep[1] + got[1].astype(f32)
     first_got = place.swap_x(first.astype(bf16))
     second_got = place.swap_y(second.astype(bf16))
     first, second = first + first_got.astype(f32), second + second_got.astype(f32)
     first_low, second_low = first.astype(bf16), second.astype(bf16)
-    if earlier:
-        first_low, second_low = lax.optimization_barrier((first_low, second_low) + earlier)[:2]
     first_got = place.swap_y(first_low)
     second_got = place.swap_x(second_low)
     own = [
@@ -278,15 +278,15 @@
 
 def qkv_body(table, normed, cosine, sine, pieces, query, own, weights, acc, sems):
     start_pieces(table, pieces, weights, sems)()
-    model = normed.shape[2]
+    count = acc.shape[0]
     acc[...] = jnp.zeros_like(acc)
 
     def one(b, _):
-        acc[...] += dims(normed[b], weights[b, :model], 1, 0)
+        acc[...] += dims(weights[b, :count], normed[b], 1, 1)
         return 0
 
     lax.fori_loop(0, normed.shape[0], one, 0)
-    flipped = acc[...].T
+    flipped = acc[...]
     head = HEAD_DIM
     heads = query.shape[0] // head
     cos, sin = cosine[...], sine[...]
@@ -354,10 +354,10 @@
     values = attended[...]
     attended_low[...] = values.astype(bf16)
     flipped = values.T.astype(bf16)
-    model = weights.shape[2]
+    first = weights.shape[1] - query.shape[0]
     keep_and_send(
         table,
-        lambda b: dims(flipped, weights[b, model:], 1, 0),
+        lambda b: dims(flipped, weights[b, first:], 1, 0),
         keep_first,
         keep_second,
         send,
@@ -391,16 +391,27 @@
     lax.fori_loop(0, count, norm, 0)
 
 
+def start_blocks(source, whole, sems):
+    def copy(b):
+        return pltpu.make_async_copy(source.at[b], whole.at[b], sems.at[b])
+
+    for b in range(source.shape[0]):
+        copy(b).start()
+    return lambda b: copy(b).wait()
+
+
 def gate_body(table, normed, pieces, active, gate_slope, up_slope, weights, acc, sems):
-    start_pieces(table, pieces, weights, sems)()
+    wait = start_blocks(pieces[0], weights, sems)
+    width = acc.shape[1]
     acc[...] = jnp.zeros_like(acc)
 
     def one(b, _):
-        acc[...] += dims(normed[b], weights[b], 1, 0)
+        wait(b)
+        acc[...] += dims(normed[b], weights[b, :width], 1, 1)
         return 0
 
     lax.fori_loop(0, normed.shape[0], one, 0)
-    half = acc.shape[1] // 2
+    half = width // 2
     rows = acc.shape[0] // 4
 
     def part(i, _):
@@ -415,58 +426,60 @@
     lax.fori_loop(0, 4, part, 0)
 
 
-def down_parts_body(table, active, grad, *parts):
-    flipped = active[...].T
-    for k, part in enumerate(parts):
-        part[...] = dims(flipped, grad[table[ORDER + k]], 1, 0).astype(bf16)
-
-
 def gate_back_body(
     table,
     grad,
     gate_slope,
     up_slope,
-    gate_pieces,
-    down_pieces,
+    pieces,
     change,
     keep_first,
     keep_second,
     send,
-    gate_weights,
-    down_weights,
+    weights,
     acc,
-    gate_sems,
-    down_sems,
+    sems,
 ):
-    down_wait = start_pieces(table, down_pieces, down_weights, down_sems)
-    gate_wait = start_pieces(table, gate_pieces, gate_weights, gate_sems)
-    down_wait()
+    wait = start_blocks(pieces[0], weights, sems)
+    half = acc.shape[1]
     acc[...] = jnp.zeros_like(acc)
 
     def one(b, _):
-        acc[...] += dims(grad[b], down_weights[b], 1, 1)
+        wait(b)
+        acc[...] += dims(grad[b], weights[b, 2 * half :], 1, 1)
         return 0
 
     lax.fori_loop(0, grad.shape[0], one, 0)
-    half = acc.shape[1]
     change[:, :half] = (acc[...] * gate_slope[...]).astype(bf16)
     change[:, half:] = (acc[...] * up_slope[...]).astype(bf16)
-    gate_wait()
     values = change[...]
     keep_and_send(
-        table, lambda b: dims(values, gate_weights[b], 1, 1), keep_first, keep_second, send
-    )
+        table, lambda b: dims(values, weights[b, : 2 * half], 1, 0), keep_first, keep_second, send
+    )
+
+
+def forward_parts_body(table, active, grad, normed, change, parts):
+    width = change.shape[1]
+    flipped = change[...].T
+    flipped_active = active[...].T
+
+    def one(b, _):
+        parts[b, :width] = dims(flipped, normed[b], 1, 0).astype(bf16)
+        parts[b, width:] = dims(flipped_active, grad[b], 1, 0).astype(bf16)
+        return 0
+
+    lax.fori_loop(0, grad.shape[0], one, 0)
 
 
 def down_body(table, active, pieces, keep_first, keep_second, send, weights, sems):
-    start_pieces(table, pieces, weights, sems)()
+    wait = start_blocks(pieces[0], weights, sems)
+    for b in range(weights.shape[0]):
+        wait(b)
     values = active[...]
-    keep_and_send(table, lambda b: dims(values, weights[b], 1, 0), keep_first, keep_second, send)
-
-
-def gate_parts_body(table, normed, change, *parts):
-    for k, part in enumerate(parts):
-        part[...] = dims(normed[table[ORDER + k]], change[...], 0, 0).astype(bf16)
+    first = weights.shape[1] - values.shape[1]
+    keep_and_send(
+        table, lambda b: dims(values, weights[b, first:], 1, 0), keep_first, keep_second, send
+    )
 
 
 def attend_back_body(
@@ -512,9 +525,10 @@
         values = grad[b].astype(f32) + scale * change[b] - hidden[b] * back
         low = values.astype(bf16)
         through[b] = low
-        return total + dims(low, weights[b, model:], 1, 1)
+        return total + dims(low, weights[b, first:], 1, 1)
 
     heads_cols = query.shape[0]
+    first = weights.shape[1] - heads_cols
     branch = lax.fori_loop(0, count, rows, jnp.zeros((tokens, heads_cols), f32))
     branch = branch.T.astype(bf16)
 
@@ -596,14 +610,53 @@
     for k, part in enumerate(parts):
         part[...] = dims(low_16, normed[table[ORDER + k]], 1, 0).astype(bf16)
     flipped = jnp.concatenate([query_low[...].T, low.T.astype(bf16)], axis=1)
-    model = weights.shape[2]
+    width = flipped.shape[1]
     keep_and_send(
         table,
-        lambda b: dims(flipped, weights[b, :model], 1, 1),
+        lambda b: dims(flipped, weights[b, :width], 1, 0),
         keep_first,
         keep_second,
         send,
     )
+
+
+def halves_of(table, whole):
+    half = whole.shape[0] // 2
+    low, high = whole[:half], whole[half:]
+    flag = table[Y] == 0
+    return jnp.where(flag, low, high), jnp.where(flag, high, low)
+
+
+def split_body(table, *refs):
+    count = len(refs) - 2
+    mine_ref, other_ref = refs[-2:]
+    at = 0
+    for i, ref in enumerate(refs[:count]):
+        whole = ref[...]
+        if i < count - 1:
+            whole = whole.T
+        mine, other = halves_of(table, whole)
+        rows = mine.shape[0]
+        mine_ref[at : at + rows] = mine
+        other_ref[at : at + rows] = other
+        at += rows
+
+
+def join_body(table, mine, got, *outs, last_turned):
+    flag = table[Y] == 0
+    at = 0
+    for i, out in enumerate(outs):
+        turned = last_turned or i < len(outs) - 1
+        rows = out.shape[1 if turned else 0] // 2
+        parts = mine[at : at + rows].astype(f32), got[at : at + rows].astype(f32)
+        at += rows
+        low, high = jnp.where(flag, parts[0], parts[1]), jnp.where(flag, parts[1], parts[0])
+        if turned:
+            out[:, :rows] = low.T
+            out[:, rows:] = high.T
+        else:
+            out[:rows] = low
+            out[rows:] = high
 
 
 def rope_tables(positions, half):
@@ -638,38 +691,21 @@
     full = (ny, tokens, width)
     wide = [(full[1:], f32), (full[1:], f32), ((2,) + full[1:], bf16)]
 
-    def by_columns(*matrices):
-        mine, other = zip(*(part_of(y, m, 1) for m in matrices))
-        got = place.swap_y(jnp.concatenate(other, axis=1))
-        return jnp.concatenate(pair(y, jnp.concatenate(mine, axis=1), got), axis=0)
-
-    def by_rows(matrix):
-        mine, other = part_of(y, matrix, 0)
+    def pieces_of(*matrices):
+        rows = sum(max(m.shape) for m in matrices) // 2
+        cols = min(matrices[0].shape)
+        mine, other = call(split_body, [((rows, cols), bf16)] * 2, table, matrices)
         return jnp.concatenate(pair(y, mine, place.swap_y(other)), axis=1)
 
-    def gathered(piece, rows_first):
-        if lined:
-            return gather_pieces(place, piece)
-        return [gather_whole(place, piece, rows_first)]
-
-    qkv_piece = by_columns(query_weight, key_matrix, value_matrix)
-    out_piece = by_rows(out_weight)
+    attend_piece = pieces_of(query_weight, key_matrix, value_matrix, out_weight)
+    forward_piece = pieces_of(gate_weight, up_weight, down_weight)
+    forward_pieces = [gather_whole(place, forward_piece)]
     if lined:
-        attend_pieces = gather_pieces(place, jnp.concatenate([qkv_piece, out_piece], axis=0))
+        attend_pieces = gather_pieces(place, attend_piece)
     else:
-        attend_pieces = [
-            jnp.concatenate(
-                [gather_whole(place, qkv_piece, True), gather_whole(place, out_piece, False)],
-                axis=1,
-            )
-        ]
-    gate_piece = by_columns(gate_weight, up_weight)
-    down_piece = by_rows(down_weight)
-    gate_pieces = gathered(after(gate_piece, attend_pieces[len(attend_pieces) // 2]), True)
-    down_pieces = gathered(after(down_piece, gate_pieces[len(gate_pieces) // 2]), False)
-    attend_shape = (ny, width + query_rows, width)
-    gate_shape = (ny, width, 2 * hidden_dev)
-    down_shape = (ny, hidden_dev, width)
+        attend_pieces = [gather_whole(place, attend_piece)]
+    attend_shape = (ny, qkv_cols + query_rows, width)
+    forward_shape = (ny, 3 * hidden_dev, width)
     sems = pltpu.SemaphoreType.DMA((ny,))
 
     def spread(value):
@@ -685,7 +721,7 @@
         [(full, bf16), (full, bf16), ((tokens, 1), f32)] + [((ny, 1, width), f32)] * 2,
         table,
         spread(layer_in) + gains,
-        earlier=[gate_piece, down_piece],
+        earlier=[forward_piece],
     )
 
     within = jnp.arange(block, dtype=jnp.int32)
@@ -697,7 +733,7 @@
         table,
         [normed_in, cosine, sine],
         [attend_pieces],
-        [pltpu.VMEM((tokens, qkv_cols), f32), sems],
+        [pltpu.VMEM((qkv_cols, tokens), f32), sems],
     )
     moved = [
         place.send_z(
@@ -718,62 +754,52 @@
         + wide,
         table,
         [query, own] + moved + [attend_weights],
-        earlier=[grad, gate_pieces[len(gate_pieces) // 4]],
-    )
-    summed = all_sum(place, (keep_first, keep_second), send, gate_pieces[len(gate_pieces) // 2])
+        earlier=[grad],
+    )
+    summed = all_sum(place, (keep_first, keep_second), send)
 
     hidden, normed_mid, inverse_mid = call(
         hidden_body,
         [(full, f32), (full, bf16), ((tokens, 1), f32)],
         table,
         [raw] + summed + [gain_mid],
-        earlier=[gate_pieces[-1], down_pieces[len(down_pieces) // 4]],
     )
     active, gate_slope, up_slope = call(
         gate_body,
         [((tokens, hidden_dev), bf16)] + [((tokens, hidden_dev), f32)] * 2,
         table,
         [normed_mid],
-        [gate_pieces],
+        [forward_pieces],
         [
-            pltpu.VMEM(gate_shape, bf16),
+            pltpu.VMEM(forward_shape, bf16),
             pltpu.VMEM((tokens, 2 * hidden_dev), f32),
             sems,
         ],
-        earlier=[down_pieces[len(down_pieces) // 2]],
-    )
-    down_parts = call(down_parts_body, [(down_shape[1:], bf16)] * ny, table, [active, grad])
+    )
     change, keep_first, keep_second, send = call(
         gate_back_body,
         [((tokens, 2 * hidden_dev), bf16)] + wide,
         table,
         [grad, gate_slope, up_slope],
-        [gate_pieces, down_pieces],
-        [
-            pltpu.VMEM(gate_shape, bf16),
-            pltpu.VMEM(down_shape, bf16),
-            pltpu.VMEM((tokens, hidden_dev), f32),
-            sems,
-            sems,
-        ],
-        earlier=[down_parts[0]],
+        [forward_pieces],
+        [pltpu.VMEM(forward_shape, bf16), pltpu.VMEM((tokens, hidden_dev), f32), sems],
     )
     summed = all_sum(place, (keep_first, keep_second), send)
+    (forward_parts,) = call(
+        forward_parts_body, [(forward_shape, bf16)], table, [active, grad, normed_mid, change]
+    )
+    forward_grad = scatter_whole(place, forward_parts)
     keep_first, keep_second, send = call(
         down_body,
         wide,
         table,
         [active],
-        [down_pieces],
-        [pltpu.VMEM(down_shape, bf16), sems],
+        [forward_pieces],
+        [pltpu.VMEM(forward_shape, bf16), sems],
         earlier=[summed[-1]],
     )
     hidden_own = own_block(place, hidden)
     layer_out = (hidden_own + own_sum(place, (keep_first, keep_second), send)).astype(bf16)
-    down_grad = scatter_sum(place, down_parts, False)
-    gate_parts = call(gate_parts_body, [(gate_shape[1:], bf16)] * ny, table, [normed_mid, change])
-    gate_grad = scatter_sum(place, gate_parts, True)
-
     through, pull, query_low, own_back, *sends = call(
         attend_back_body,
         [
@@ -817,7 +843,7 @@
         table,
         [query_low, normed_in, attended_low, through],
     )
-    query_grad = scatter_sum(place, query_parts, False)
+    query_grad = scatter_sum(place, query_parts)
 
     moved = [
         place.send_z(
@@ -832,7 +858,7 @@
         table,
         [own_back] + moved + [query_low, normed_in, attend_weights, cosine, sine],
     )
-    kv_grad = scatter_sum(place, kv_parts, False)
+    kv_grad = scatter_sum(place, kv_parts)
     first_own = own_sum(place, (keep_first, keep_second), send)
     input_own = layer_in.astype(f32)
     inverse_own, _ = part_of(y, inverse_in, 0)
@@ -850,30 +876,30 @@
         terms = terms + place.swap_gx(terms, bit)
         bit *= 2
 
-    def joined(summed_part, axis):
-        mine, other = part_of(y, summed_part, axis)
-        return pair(y, mine, place.swap_y(other.astype(bf16)).astype(f32))
-
-    gate_low, gate_high = joined(gate_grad, 0)
-    down_grad = jnp.concatenate(joined(down_grad, 1), axis=0)
-    query_low, query_high = joined(query_grad, 1)
-    kv_low, kv_high = joined(kv_grad, 1)
-
-    def stacked(low, high, start, stop):
-        return jnp.concatenate([low[start:stop], high[start:stop]], axis=0)
-
-    half_kv = kv_rows // 2
+    def joined(summed_part, outs, last_turned=False):
+        mine, other = part_of(y, summed_part, 1)
+        got = place.swap_y(other.astype(bf16))
+        return call(
+            partial(join_body, last_turned=last_turned),
+            [(m.shape, f32) for m in outs],
+            table,
+            [mine, got],
+        )
+
+    gate_grad, up_grad, down_grad = joined(forward_grad, (gate_weight, up_weight, down_weight))
+    query_out, out_out = joined(query_grad, (query_weight, out_weight))
+    key_out, value_out = joined(kv_grad, (key_matrix, value_matrix), True)
     return (
         layer_out,
         in_grad,
         terms[0],
-        stacked(query_low, query_high, 0, query_rows).T,
-        stacked(kv_low, kv_high, 0, half_kv).T,
-        stacked(kv_low, kv_high, half_kv, kv_rows).T,
-        stacked(query_low, query_high, query_rows, 2 * query_rows),
+        query_out,
+        key_out,
+        value_out,
+        out_out,
         terms[1],
-        jnp.concatenate([gate_low[:, :hidden_dev], gate_high[:, :hidden_dev]], axis=1),
-        jnp.concatenate([gate_low[:, hidden_dev:], gate_high[:, hidden_dev:]], axis=1),
+        gate_grad,
+        up_grad,
         down_grad,
     )
 

time: 459 us -> 440 us (0.959)
  starting transfers between devices: 97.6 us -> 72.2 us
  waiting for transfers between devices: 259 us -> 245 us
  between operations: 2 us -> 15.2 us
  local copies, waits for them, and re-layouts: 20.3 us -> 31.1 us
  other arithmetic: 30.9 us -> 22.6 us
    ppermute x34 -> x18, waiting for transfers between devices: 172 us -> 132 us  [send_z(): return lax.ppermute(value, 'gx', pairs)]
    ppermute x34 -> x18, starting transfers between devices: 59.3 us -> 28.5 us  [send_z(): return lax.ppermute(value, 'gx', pairs)]
    ppermute x21 -> x18, waiting for transfers between devices: 55.3 us -> 78.4 us  [swap_gx(): return lax.ppermute(value, 'gx', [(i, i ^ bit) for i in range(self.nx)])]
    unnamed x146 -> x145, local copies, waits for them, and re-layouts: 15.4 us -> 29.2 us
    ppermute x19, waiting for transfers between devices: 2.18 us -> 8.8 us  [swap_c(): return lax.ppermute(value, 'gy', [(i, i ^ 1) for i in range(self.ny)])]
    ppermute x21 -> x18, starting transfers between devices: 22.8 us -> 27.6 us  [swap_gx(): return lax.ppermute(value, 'gx', [(i, i ^ bit) for i in range(self.nx)])]
    pallas_call x13 -> x17, Pallas kernels: 48.4 us -> 52.9 us  [call(): pl.pallas_call(kernel, out_shape=[jax.ShapeDtypeStruct(shape, dtype) for...]
  transfers between devices with their start and end apart: 84 -> 67, of which waited for: 39 -> 37; matrix products, arithmetic and copies ran while one was open for 9% -> 5% of each run, Pallas kernels for 5% -> 8%
where the time goes in v1:
time: 440 us; the launch traced here: 439 us
  waiting for transfers between devices  245 us (56%)
  starting transfers between devices  72.2 us (16%)
  Pallas kernels  52.9 us (12%)
  local copies, waits for them, and re-layouts  31.1 us (7%)
  other arithmetic  22.6 us (5%)
  between operations  15.2 us (3%)
    ppermute x18, waiting for transfers between devices, send_z(): return lax.ppermute(value, 'gx', pairs)  132 us
    ppermute x18, waiting for transfers between devices, swap_gx(): return lax.ppermute(value, 'gx', [(i, i ^ bit) for i in range(self.nx)])  78.4 us
    pallas_call x17, Pallas kernels, call(): pl.pallas_call(kernel, out_shape=[jax.ShapeDtypeStruct(shape, dtype) for...  52.9 us
    unnamed x145, local copies, waits for them, and re-layouts  29.2 us
    ppermute x18, starting transfers between devices, send_z(): return lax.ppermute(value, 'gx', pairs)  28.5 us
    ppermute x18, starting transfers between devices, swap_gx(): return lax.ppermute(value, 'gx', [(i, i ^ bit) for i in range(self.nx)])  27.6 us
    ppermute x10, waiting for transfers between devices, swap_x(): return lax.ppermute(value, 'gy', [(i, i ^ 2) for i in range(self.ny)])  26.6 us
    ppermute x10, starting transfers between devices, swap_x(): return lax.ppermute(value, 'gy', [(i, i ^ 2) for i in range(self.ny)])  13.3 us
  transfers between devices with their start and end apart: 67, of which 37 were waited for; matrix products, arithmetic and copies ran while one was open for 5% of the time, Pallas kernels for 8%

profile of v1, /device:TPU:0, one launch (start us, length us, event | category | flops | bytes accessed | tf_op | source)
XLA Modules:
  0.0 439.4 jit_solution(8412922854698005397)
XLA Ops:
  11.8 3.0 collective-permute-start.10
  14.8 13.3 %collective-permute-done.10 = bf16[1536,192]{0,1:T(8,128)(2,1)S(1)} collective-permute-done((bf16[1536,192]{0,1:T(8,128)(2,1)S(1)}, bf16[1536,192]{0,1:T(8,128)(2,1)S(1)}, u32[]{:S(2)}, u32[]{:S(2)}) %collective-permute-start.10) | collective-permute-done | bytes 589856 | tf_op jit(solution)/shard_map/ppermute | solution.py:51
  34.5 5.0 %collective-permute-done.11 = bf16[576,192]{1,0:T(8,128)(2,1)S(1)} collective-permute-done((bf16[576,192]{1,0:T(8,128)(2,1)S(1)}, bf16[576,192]{1,0:T(8,128)(2,1)S(1)}, u32[]{:S(2)}, u32[]{:S(2)}) %collective-permute-start.11) | collective-permute-done | bytes 221216 | tf_op jit(solution)/shard_map/ppermute | solution.py:51
  57.8 25.6 %collective-permute-done.13.refs_5_ = bf16[576,384]{1,0:T(8,128)(2,1)S(1)} collective-permute-done((bf16[576,384]{1,0:T(8,128)(2,1)S(1)}, bf16[576,384]{1,0:T(8,128)(2,1)S(1)}, u32[]{:S(2)}, u32[]{:S(2)}) %collective-permute-start.13) | collective-permute-done | bytes 442400 | tf_op jit(solution)/shard_map/ppermute | solution.py:64
  86.4 6.7 %collective-permute-done.12.refs_4_ = bf16[576,384]{1,0:T(8,128)(2,1)S(1)} collective-permute-done((bf16[576,384]{1,0:T(8,128)(2,1)S(1)}, bf16[576,384]{1,0:T(8,128)(2,1)S(1)}, u32[]{:S(2)}, u32[]{:S(2)}) %collective-permute-start.12) | collective-permute-done | bytes 442400 | tf_op jit(solution)/shard_map/ppermute | solution.py:64
  94.8 5.6 %collective-permute-done.21.refs_3_ = bf16[256,384]{1,0:T(8,128)(2,1)S(1)} collective-permute-done((bf16[256,384]{1,0:T(8,128)(2,1)S(1)}, bf16[256,384]{1,0:T(8,128)(2,1)S(1)}, u32[]{:S(2)}, u32[]{:S(2)}) %collective-permute-start.21) | collective-permute-done | bytes 196640 | tf_op jit(solution)/shard_map/ppermute | solution.py:51
  100.4 18.9 %collective-permute-done.15.refs_7_ = bf16[576,384]{1,0:T(8,128)(2,1)S(1)} collective-permute-done((bf16[576,384]{1,0:T(8,128)(2,1)S(1)}, bf16[576,384]{1,0:T(8,128)(2,1)S(1)}, u32[]{:S(2)}, u32[]{:S(2)}) %collective-permute-start.15) | collective-permute-done | bytes 442400 | tf_op jit(solution)/shard_map/ppermute | solution.py:64
  119.3 3.3 shard_map.197
  129.4 4.5 %collective-permute-done.16.refs_2_ = bf16[192,512]{1,0:T(8,128)(2,1)S(1)} collective-permute-done((bf16[192,512]{1,0:T(8,128)(2,1)S(1)}, bf16[192,512]{1,0:T(8,128)(2,1)S(1)}, u32[]{:S(2)}, u32[]{:S(2)}) %collective-permute-start.16) | collective-permute-done | bytes 196640 | tf_op jit(solution)/shard_map/ppermute | solution.py:64
  133.8 8.4 %collective-permute-done.17.refs_3_ = bf16[192,512]{1,0:T(8,128)(2,1)S(1)} collective-permute-done((bf16[192,512]{1,0:T(8,128)(2,1)S(1)}, bf16[192,512]{1,0:T(8,128)(2,1)S(1)}, u32[]{:S(2)}, u32[]{:S(2)}) %collective-permute-start.17) | collective-permute-done | bytes 196640 | tf_op jit(solution)/shard_map/ppermute | solution.py:64
  142.3 5.9 %collective-permute-done.18.refs_4_ = bf16[192,512]{1,0:T(8,128)(2,1)S(1)} collective-permute-done((bf16[192,512]{1,0:T(8,128)(2,1)S(1)}, bf16[192,512]{1,0:T(8,128)(2,1)S(1)}, u32[]{:S(2)}, u32[]{:S(2)}) %collective-permute-start.18) | collective-permute-done | bytes 196640 | tf_op jit(solution)/shard_map/ppermute | solution.py:64
  148.2 5.7 %shard_map.199 = (f32[192,512]{1,0:T(8,128)S(1)}, bf16[192,512]{1,0:T(8,128)(2,1)S(1)}, f32[2,1,512]{2,1,0:T(1,128)S(1)}, bf16[192,1024]{1,0:T(8,128)(2,1)S(1)},...) custom-call(s32[11]{0:T(128)S(1)} %concatenate.9.table_ref, ...), custom_call_target="tpu_custom_call" | custom-call | tf_op jit(solution)/shard_map/pallas_call | solution.py:177
  157.9 9.6 %collective-permute-done.29 = bf16[512,384]{1,0:T(8,128)(2,1)S(1)} collective-permute-done((bf16[512,384]{1,0:T(8,128)(2,1)S(1)}, bf16[512,384]{1,0:T(8,128)(2,1)S(1)}, u32[]{:S(2)}, u32[]{:S(2)}) %collective-permute-start.29) | collective-permute-done | bytes 393248 | tf_op jit(solution)/shard_map/ppermute | solution.py:51
  169.8 10.0 %collective-permute-done.30 = bf16[512,384]{1,0:T(8,128)(2,1)S(1)} collective-permute-done((bf16[512,384]{1,0:T(8,128)(2,1)S(1)}, bf16[512,384]{1,0:T(8,128)(2,1)S(1)}, u32[]{:S(2)}, u32[]{:S(2)}) %collective-permute-start.30) | collective-permute-done | bytes 393248 | tf_op jit(solution)/shard_map/ppermute | solution.py:57
  179.9 6.7 %collective-permute-done.27 = bf16[512,384]{1,0:T(8,128)(2,1)S(1)} collective-permute-done((bf16[512,384]{1,0:T(8,128)(2,1)S(1)}, bf16[512,384]{1,0:T(8,128)(2,1)S(1)}, u32[]{:S(2)}, u32[]{:S(2)}) %collective-permute-start.27) | collective-permute-done | bytes 393248 | tf_op jit(solution)/shard_map/ppermute | solution.py:57
  188.4 7.9 %collective-permute-done.28 = bf16[512,384]{1,0:T(8,128)(2,1)S(1)} collective-permute-done((bf16[512,384]{1,0:T(8,128)(2,1)S(1)}, bf16[512,384]{1,0:T(8,128)(2,1)S(1)}, u32[]{:S(2)}, u32[]{:S(2)}) %collective-permute-start.28) | collective-permute-done | bytes 393248 | tf_op jit(solution)/shard_map/ppermute | solution.py:51
  207.5 5.1 %shard_map.201 = (bf16[512,512]{1,0:T(8,128)(2,1)S(1)}, f32[512,512]{1,0:T(8,128)S(1)}, f32[512,512]{1,0:T(8,128)S(1)}) custom-call(s32[11]{0:T(128)S(1)} %concatenate.9.table_ref, bf16[4,512,384]{2,1,0:T(8,128)(2,1)S(1)} %copy-done.11, bf16[4,1536,384]{2,1,0:T(8,128)(2,1)S(1)} %bitcast.93), custom_call_target="tpu_custom_call" | custom-call | tf_op jit(solution)/shard_map/pallas_call | solution.py:177
  212.6 6.2 %shard_map.202 = (bf16[512,1024]{1,0:T(8,128)(2,1)S(1)}, f32[512,384]{1,0:T(8,128)S(1)}, f32[512,384]{1,0:T(8,128)S(1)}, bf16[2,512,384]{2,1,0:T(8,128)(2,1)S(1)}) custom-call(s32[11]{0:T(128)S(1)} %concatenate.9.table_ref, bf16[4,512,384]{2,1,0:T(8,128)(2,1)S(1)} %shard_map.198.refs_6_.refs_0_.refs_1_, f32[512,512]{1,0:T(8,128)S(1)} %get-tuple-element.85.refs_1_, ...), custom_call_target="tpu_custom_call" | custom-call | tf_op jit(solution)/shard_map/pallas_call | solution.py:177
  221.4 4.9 %shard_map.209 = bf16[4,1536,384]{2,1,0:T(8,128)(2,1)S(1)} custom-call(s32[11]{0:T(128)S(1)} %concatenate.9.table_ref, bf16[512,512]{1,0:T(8,128)(2,1)S(1)} %get-tuple-element.84.refs_0_, bf16[4,512,384]{2,1,0:T(8,128)(2,1)S(1)} %shard_map.198.refs_6_.refs_0_.refs_1_, bf16[4,512,384]{2,1,0:T(8,128)(2,1)S(1)} %copy-done.12, ...), custom_call_target="tpu_custom_call" | custom-call | tf_op jit(solution)/shard_map/pallas_call | solution.py:177
  236.2 8.1 %collective-permute-done.34 = bf16[512,384]{1,0:T(8,128)(2,1)S(1)} collective-permute-done((bf16[512,384]{1,0:T(8,128)(2,1)S(1)}, bf16[512,384]{1,0:T(8,128)(2,1)S(1)}, u32[]{:S(2)}, u32[]{:S(2)}) %collective-permute-start.34) | collective-permute-done | bytes 393248 | tf_op jit(solution)/shard_map/ppermute | solution.py:51
  248.8 8.3 %collective-permute-done.41 = bf16[512,384]{1,0:T(8,128)(2,1)} collective-permute-done((bf16[512,384]{1,0:T(8,128)(2,1)}, bf16[512,384]{1,0:T(8,128)(2,1)}, u32[]{:S(2)}, u32[]{:S(2)}) %collective-permute-start.41) | collective-permute-done | bytes 393248 | tf_op jit(solution)/shard_map/ppermute | solution.py:51
  257.4 3.2 broadcast_select_fusion.4
  263.0 8.3 %shard_map.204 = (bf16[4,512,384]{2,1,0:T(8,128)(2,1)S(1)}, f32[512,1]{1,0:T(8,128)S(1)}, bf16[192,512]{1,0:T(8,128)(2,1)S(1)}, f32[192,512]{1,0:T(8,128)S(1)}, ...) custom-call(s32[11]{0:T(128)S(1)} %concatenate.9.table_ref, ...), custom_call_target="tpu_custom_call" | custom-call | tf_op jit(solution)/shard_map/pallas_call | solution.py:177
  279.5 22.8 %collective-permute-done.43.refs_1_ = bf16[192,512]{1,0:T(8,128)(2,1)S(1)} collective-permute-done((bf16[192,512]{1,0:T(8,128)(2,1)}, bf16[192,512]{1,0:T(8,128)(2,1)S(1)}, u32[]{:S(2)}, u32[]{:S(2)}) %collective-permute-start.43) | collective-permute-done | bytes 196640 | tf_op jit(solution)/shard_map/ppermute | solution.py:64
  302.3 27.8 %collective-permute-done.44.refs_2_ = bf16[192,512]{1,0:T(8,128)(2,1)S(1)} collective-permute-done((bf16[192,512]{1,0:T(8,128)(2,1)}, bf16[192,512]{1,0:T(8,128)(2,1)S(1)}, u32[]{:S(2)}, u32[]{:S(2)}) %collective-permute-start.44) | collective-permute-done | bytes 196640 | tf_op jit(solution)/shard_map/ppermute | solution.py:64
  346.3 4.0 shard_map.203
  355.8 3.6 collective-permute-start.54
  374.1 3.3 collective-permute-done.57
  380.1 3.4 collective-permute-done.48
  398.6 3.9 collective-permute-done.38
  403.8 3.2 collective-permute-start.52
  413.7 13.1 %collective-permute-done.39 = bf16[256,384]{1,0:T(8,128)(2,1)S(1)} collective-permute-done((bf16[256,384]{1,0:T(8,128)(2,1)S(1)}, bf16[256,384]{1,0:T(8,128)(2,1)S(1)}, u32[]{:S(2)}, u32[]{:S(2)}) %collective-permute-start.39) | collective-permute-done | bytes 196640 | tf_op jit(solution)/shard_map/ppermute | solution.py:51
  (322 shorter events, 154.9 us)
Async XLA Ops:
  7.2 196.6 %all-gather.3.cloned.1.call-start = ((), (), s32[]{:S(2)}) async-start(), calls=%async_computation.2 | async-start | bytes 5898240 | tf_op jit(solution)/shard_map/all_gather | solution.py:98
  11.8 16.4 %collective-permute-start.10 = (bf16[1536,192]{0,1:T(8,128)(2,1)S(1)}, bf16[1536,192]{0,1:T(8,128)(2,1)S(1)}, u32[]{:S(2)}, u32[]{:S(2)}) collective-permute-start(bf16[1536,192]{0,1:T(8,128)(2,1)S(1)} %copy.44), channel_id=1, source_target_pairs={{0,4},{4,0},{8,12},{12,8},{16,20},{20,16},{24,28},{28,24},{1,5},{5... | collective-permute-start | bytes 1769480 | tf_op jit(solution)/shard_map/ppermute | solution.py:51
  30.2 376.8 %reduce-scatter.2.cloned.1.call-start = ((), (), s32[]{:S(2)}) async-start(), calls=%async_computation.1 | async-start | bytes 5898240 | tf_op jit(solution)/shard_map/reduce_scatter | solution.py:113
  39.7 43.7 %collective-permute-start.13 = (bf16[576,384]{1,0:T(8,128)(2,1)S(1)}, bf16[576,384]{1,0:T(8,128)(2,1)S(1)}, u32[]{:S(2)}, u32[]{:S(2)}) collective-permute-start(bf16[576,384]{1,0:T(8,128)(2,1)S(1)} %pad_maximum_fusion.1.refs_3_), channel_id=1, source_target_pairs={{0,16},{4,20},{8,24},{12,28},{16,0},{20,4},{24,8},{28,12},{1,17},{... | collective-permute-start | bytes 1327112 | tf_op jit(solution)/shard_map/ppermute | solution.py:64
  51.0 42.0 %collective-permute-start.12 = (bf16[576,384]{1,0:T(8,128)(2,1)S(1)}, bf16[576,384]{1,0:T(8,128)(2,1)S(1)}, u32[]{:S(2)}, u32[]{:S(2)}) collective-permute-start(bf16[576,384]{1,0:T(8,128)(2,1)S(1)} %pad_maximum_fusion.1.refs_3_), channel_id=1, source_target_pairs={{0,8},{4,12},{8,0},{12,4},{16,24},{20,28},{24,16},{28,20},{1,9},{5... | collective-permute-start | bytes 1327112 | tf_op jit(solution)/shard_map/ppermute | solution.py:64
  52.6 41.2 %collective-permute-start.14 = (bf16[576,384]{1,0:T(8,128)(2,1)S(1)}, bf16[576,384]{1,0:T(8,128)(2,1)S(1)}, u32[]{:S(2)}, u32[]{:S(2)}) collective-permute-start(bf16[576,384]{1,0:T(8,128)(2,1)S(1)} %pad_maximum_fusion.1.refs_3_), channel_id=1, source_target_pairs={{8,16},{12,20},{16,8},{20,12},{9,17},{13,21},{17,9},{21,13},{10,18... | collective-permute-start | bytes 1327112 | tf_op jit(solution)/shard_map/ppermute | solution.py:64
  56.3 36.8 %collective-permute-start.19 = (bf16[256,384]{1,0:T(8,128)(2,1)S(1)}, bf16[256,384]{1,0:T(8,128)(2,1)S(1)}, u32[]{:S(2)}, u32[]{:S(2)}) collective-permute-start(bf16[256,384]{1,0:T(8,128)(2,1)S(1)} %copy-done.40), channel_id=1, source_target_pairs={{0,2},{1,3},{2,0},{3,1},{4,6},{5,7},{6,4},{7,5},{8,10},{9,11},{10,... | collective-permute-start | bytes 589832 | tf_op jit(solution)/shard_map/ppermute | solution.py:57
  83.4 35.9 %collective-permute-start.15 = (bf16[576,384]{1,0:T(8,128)(2,1)S(1)}, bf16[576,384]{1,0:T(8,128)(2,1)S(1)}, u32[]{:S(2)}, u32[]{:S(2)}) collective-permute-start(bf16[576,384]{1,0:T(8,128)(2,1)S(1)} %collective-permute-done.13.refs_5_), channel_id=1, source_target_pairs={{8,0},{12,4},{16,24},{20,28},{9,1},{13,5},{17,25},{21,29},{10,2},{... | collective-permute-start | bytes 1327112 | tf_op jit(solution)/shard_map/ppermute | solution.py:64
  93.1 31.4 %collective-permute-start.22 = (bf16[256,384]{1,0:T(8,128)(2,1)S(1)}, bf16[256,384]{1,0:T(8,128)(2,1)S(1)}, u32[]{:S(2)}, u32[]{:S(2)}) collective-permute-start(bf16[256,384]{1,0:T(8,128)(2,1)S(1)} %copy-done.40), channel_id=1, source_target_pairs={{0,1},{1,0},{2,3},{3,2},{4,5},{5,4},{6,7},{7,6},{8,9},{9,8},{10,11... | collective-permute-start | bytes 589832 | tf_op jit(solution)/shard_map/ppermute | solution.py:60
  93.8 33.6 %collective-permute-start.23 = (bf16[256,384]{1,0:T(8,128)(2,1)S(1)}, bf16[256,384]{1,0:T(8,128)(2,1)S(1)}, u32[]{:S(2)}, u32[]{:S(2)}) collective-permute-start(bf16[256,384]{1,0:T(8,128)(2,1)S(1)} %collective-permute-done.19.refs_1_), channel_id=1, source_target_pairs={{0,1},{1,0},{2,3},{3,2},{4,5},{5,4},{6,7},{7,6},{8,9},{9,8},{10,11... | collective-permute-start | bytes 589832 | tf_op jit(solution)/shard_map/ppermute | solution.py:60
  94.5 34.2 %collective-permute-start.24 = (bf16[256,384]{1,0:T(8,128)(2,1)S(1)}, bf16[256,384]{1,0:T(8,128)(2,1)S(1)}, u32[]{:S(2)}, u32[]{:S(2)}) collective-permute-start(bf16[256,384]{1,0:T(8,128)(2,1)S(1)} %collective-permute-done.20.refs_2_), channel_id=1, source_target_pairs={{0,1},{1,0},{2,3},{3,2},{4,5},{5,4},{6,7},{7,6},{8,9},{9,8},{10,11... | collective-permute-start | bytes 589832 | tf_op jit(solution)/shard_map/ppermute | solution.py:60
  100.4 28.3 %collective-permute-start.25 = (bf16[256,384]{1,0:T(8,128)(2,1)S(1)}, bf16[256,384]{1,0:T(8,128)(2,1)S(1)}, u32[]{:S(2)}, u32[]{:S(2)}) collective-permute-start(bf16[256,384]{1,0:T(8,128)(2,1)S(1)} %collective-permute-done.21.refs_3_), channel_id=1, source_target_pairs={{0,1},{1,0},{2,3},{3,2},{4,5},{5,4},{6,7},{7,6},{8,9},{9,8},{10,11... | collective-permute-start | bytes 589832 | tf_op jit(solution)/shard_map/ppermute | solution.py:60
  122.7 11.2 %collective-permute-start.16 = (bf16[192,512]{1,0:T(8,128)(2,1)S(1)}, bf16[192,512]{1,0:T(8,128)(2,1)S(1)}, u32[]{:S(2)}, u32[]{:S(2)}) collective-permute-start(bf16[192,512]{1,0:T(8,128)(2,1)S(1)} %get-tuple-element.75.refs_1_.refs_10_), channel_id=1, source_target_pairs={{0,8},{4,12},{8,16},{12,20},{1,9},{5,13},{9,17},{13,21},{2,10},{6,... | collective-permute-start | bytes 589832 | tf_op jit(solution)/shard_map/ppermute | solution.py:64
  124.4 17.8 %collective-permute-start.17 = (bf16[192,512]{1,0:T(8,128)(2,1)S(1)}, bf16[192,512]{1,0:T(8,128)(2,1)S(1)}, u32[]{:S(2)}, u32[]{:S(2)}) collective-permute-start(bf16[192,512]{1,0:T(8,128)(2,1)S(1)} %get-tuple-element.75.refs_1_.refs_10_), channel_id=1, source_target_pairs={{0,16},{4,20},{8,24},{12,28},{1,17},{5,21},{9,25},{13,29},{2,18},{... | collective-permute-start | bytes 589832 | tf_op jit(solution)/shard_map/ppermute | solution.py:64
  127.3 20.8 %collective-permute-start.18 = (bf16[192,512]{1,0:T(8,128)(2,1)S(1)}, bf16[192,512]{1,0:T(8,128)(2,1)S(1)}, u32[]{:S(2)}, u32[]{:S(2)}) collective-permute-start(bf16[192,512]{1,0:T(8,128)(2,1)S(1)} %get-tuple-element.75.refs_1_.refs_10_), channel_id=1, source_target_pairs={{0,24},{4,28},{1,25},{5,29},{2,26},{6,30},{3,27},{7,31}} | collective-permute-start | bytes 589832 | tf_op jit(solution)/shard_map/ppermute | solution.py:64
  156.3 11.2 %collective-permute-start.29 = (bf16[512,384]{1,0:T(8,128)(2,1)S(1)}, bf16[512,384]{1,0:T(8,128)(2,1)S(1)}, u32[]{:S(2)}, u32[]{:S(2)}) collective-permute-start(bf16[512,384]{1,0:T(8,128)(2,1)S(1)} %fusion.16), channel_id=1, source_target_pairs={{0,4},{4,0},{8,12},{12,8},{16,20},{20,16},{24,28},{28,24},{1,5},{5... | collective-permute-start | bytes 1179656 | tf_op jit(solution)/shard_map/ppermute | solution.py:51
  167.7 12.1 %collective-permute-start.30 = (bf16[512,384]{1,0:T(8,128)(2,1)S(1)}, bf16[512,384]{1,0:T(8,128)(2,1)S(1)}, u32[]{:S(2)}, u32[]{:S(2)}) collective-permute-start(bf16[512,384]{1,0:T(8,128)(2,1)S(1)} %get-tuple-element.189), channel_id=1, source_target_pairs={{0,2},{1,3},{2,0},{3,1},{4,6},{5,7},{6,4},{7,5},{8,10},{9,11},{10,... | collective-permute-start | bytes 1179656 | tf_op jit(solution)/shard_map/ppermute | solution.py:57
  169.3 17.3 %collective-permute-start.27 = (bf16[512,384]{1,0:T(8,128)(2,1)S(1)}, bf16[512,384]{1,0:T(8,128)(2,1)S(1)}, u32[]{:S(2)}, u32[]{:S(2)}) collective-permute-start(bf16[512,384]{1,0:T(8,128)(2,1)S(1)} %get-tuple-element.190), channel_id=1, source_target_pairs={{0,2},{1,3},{2,0},{3,1},{4,6},{5,7},{6,4},{7,5},{8,10},{9,11},{10,... | collective-permute-start | bytes 1179656 | tf_op jit(solution)/shard_map/ppermute | solution.py:57
  233.1 11.2 %collective-permute-start.34 = (bf16[512,384]{1,0:T(8,128)(2,1)S(1)}, bf16[512,384]{1,0:T(8,128)(2,1)S(1)}, u32[]{:S(2)}, u32[]{:S(2)}) collective-permute-start(bf16[512,384]{1,0:T(8,128)(2,1)S(1)} %get-tuple-element.185), channel_id=1, source_target_pairs={{0,4},{4,0},{8,12},{12,8},{16,20},{20,16},{24,28},{28,24},{1,5},{5... | collective-permute-start | bytes 1179656 | tf_op jit(solution)/shard_map/ppermute | solution.py:51
  274.6 27.7 %collective-permute-start.43 = (bf16[192,512]{1,0:T(8,128)(2,1)}, bf16[192,512]{1,0:T(8,128)(2,1)S(1)}, u32[]{:S(2)}, u32[]{:S(2)}) collective-permute-start(bf16[192,512]{1,0:T(8,128)(2,1)} %get-tuple-element.100), channel_id=1, source_target_pairs={{8,0},{12,4},{16,8},{20,12},{9,1},{13,5},{17,9},{21,13},{10,2},{14... | collective-permute-start | bytes 589832 | tf_op jit(solution)/shard_map/ppermute | solution.py:64
  275.9 54.3 %collective-permute-start.44 = (bf16[192,512]{1,0:T(8,128)(2,1)}, bf16[192,512]{1,0:T(8,128)(2,1)S(1)}, u32[]{:S(2)}, u32[]{:S(2)}) collective-permute-start(bf16[192,512]{1,0:T(8,128)(2,1)} %get-tuple-element.101), channel_id=1, source_target_pairs={{16,0},{20,4},{24,8},{28,12},{17,1},{21,5},{25,9},{29,13},{18,2},{... | collective-permute-start | bytes 589832 | tf_op jit(solution)/shard_map/ppermute | solution.py:64
  277.2 53.0 %collective-permute-start.45 = (bf16[192,512]{1,0:T(8,128)(2,1)}, bf16[192,512]{1,0:T(8,128)(2,1)S(1)}, u32[]{:S(2)}, u32[]{:S(2)}) collective-permute-start(bf16[192,512]{1,0:T(8,128)(2,1)} %get-tuple-element.102), channel_id=1, source_target_pairs={{24,0},{28,4},{25,1},{29,5},{26,2},{30,6},{27,3},{31,7}} | collective-permute-start | bytes 589832 | tf_op jit(solution)/shard_map/ppermute | solution.py:64
  337.7 13.8 %collective-permute-start.61 = (bf16[192,384]{1,0:T(8,128)(2,1)S(1)}, bf16[192,384]{1,0:T(8,128)(2,1)S(1)}, u32[]{:S(2)}, u32[]{:S(2)}) collective-permute-start(bf16[192,384]{1,0:T(8,128)(2,1)S(1)} %get-tuple-element.116), channel_id=1, source_target_pairs={{0,8},{4,12},{24,16},{28,20},{1,9},{5,13},{25,17},{29,21},{2,10},{... | collective-permute-start | bytes 442376 | tf_op jit(solution)/shard_map/ppermute | solution.py:64
  341.2 12.9 %collective-permute-start.56 = (bf16[384,384]{1,0:T(8,128)(2,1)S(1)}, bf16[384,384]{1,0:T(8,128)(2,1)S(1)}, u32[]{:S(2)}, u32[]{:S(2)}) collective-permute-start(bf16[384,384]{1,0:T(8,128)(2,1)S(1)} %get-tuple-element.111), channel_id=1, source_target_pairs={{0,8},{4,12},{24,16},{28,20},{1,9},{5,13},{25,17},{29,21},{2,10},{... | collective-permute-start | bytes 884744 | tf_op jit(solution)/shard_map/ppermute | solution.py:64
  342.5 28.8 %collective-permute-start.55 = (bf16[384,384]{1,0:T(8,128)(2,1)S(1)}, bf16[384,384]{1,0:T(8,128)(2,1)S(1)}, u32[]{:S(2)}, u32[]{:S(2)}) collective-permute-start(bf16[384,384]{1,0:T(8,128)(2,1)S(1)} %get-tuple-element.111), channel_id=1, source_target_pairs={{8,16},{12,20},{16,8},{20,12},{9,17},{13,21},{17,9},{21,13},{10,18... | collective-permute-start | bytes 884744 | tf_op jit(solution)/shard_map/ppermute | solution.py:64
  351.2 15.5 %collective-permute-start.46 = (bf16[2,512,384]{2,1,0:T(8,128)(2,1)S(1)}, bf16[2,512,384]{2,1,0:T(8,128)(2,1)S(1)}, u32[]{:S(2)}, u32[]{:S(2)}) collective-permute-start(bf16[2,512,384]{2,1,0:T(8,128)(2,1)S(1)} %get-tuple-element.105), channel_id=1, source_target_pairs={{0,1},{1,0},{2,3},{3,2},{4,5},{5,4},{6,7},{7,6},{8,9},{9,8},{10,11... | collective-permute-start | bytes 2359304 | tf_op jit(solution)/shard_map/ppermute | solution.py:60
  355.8 18.3 %collective-permute-start.54 = (bf16[384,384]{1,0:T(8,128)(2,1)S(1)}, bf16[384,384]{1,0:T(8,128)(2,1)S(1)}, u32[]{:S(2)}, u32[]{:S(2)}) collective-permute-start(bf16[384,384]{1,0:T(8,128)(2,1)S(1)} %get-tuple-element.110), channel_id=1, source_target_pairs={{0,8},{4,12},{8,0},{12,4},{16,24},{20,28},{24,16},{28,20},{1,9},{5... | collective-permute-start | bytes 884744 | tf_op jit(solution)/shard_map/ppermute | solution.py:64
  361.5 15.8 %collective-permute-start.57 = (bf16[384,384]{1,0:T(8,128)(2,1)S(1)}, bf16[384,384]{1,0:T(8,128)(2,1)S(1)}, u32[]{:S(2)}, u32[]{:S(2)}) collective-permute-start(bf16[384,384]{1,0:T(8,128)(2,1)S(1)} %add_convert_fusion.4), channel_id=1, source_target_pairs={{0,16},{4,20},{8,24},{12,28},{16,0},{20,4},{24,8},{28,12},{1,17},{... | collective-permute-start | bytes 884744 | tf_op jit(solution)/shard_map/ppermute | solution.py:64
  369.8 20.7 %collective-permute-start.37 = (bf16[2,512,384]{2,1,0:T(8,128)(2,1)}, bf16[2,512,384]{2,1,0:T(8,128)(2,1)}, u32[]{:S(2)}, u32[]{:S(2)}) collective-permute-start(bf16[2,512,384]{2,1,0:T(8,128)(2,1)} %get-tuple-element.90), channel_id=1, source_target_pairs={{0,1},{1,0},{2,3},{3,2},{4,5},{5,4},{6,7},{7,6},{8,9},{9,8},{10,11... | collective-permute-start | bytes 2359304 | tf_op jit(solution)/shard_map/ppermute | solution.py:60
  409.0 20.1 %collective-permute-start.64 = (bf16[1536,192]{0,1:T(8,128)(2,1)S(1)}, bf16[1536,192]{0,1:T(8,128)(2,1)S(1)}, u32[]{:S(2)}, u32[]{:S(2)}) collective-permute-start(bf16[1536,192]{0,1:T(8,128)(2,1)S(1)} %copy.50), channel_id=1, source_target_pairs={{0,4},{4,0},{8,12},{12,8},{16,20},{20,16},{24,28},{28,24},{1,5},{5... | collective-permute-start | bytes 1769480 | tf_op jit(solution)/shard_map/ppermute | solution.py:51
  410.6 16.2 %collective-permute-start.39 = (bf16[256,384]{1,0:T(8,128)(2,1)S(1)}, bf16[256,384]{1,0:T(8,128)(2,1)S(1)}, u32[]{:S(2)}, u32[]{:S(2)}) collective-permute-start(bf16[256,384]{1,0:T(8,128)(2,1)S(1)} %select_convert_fusion.4), channel_id=1, source_target_pairs={{0,4},{4,0},{8,12},{12,8},{16,20},{20,16},{24,28},{28,24},{1,5},{5... | collective-permute-start | bytes 589832 | tf_op jit(solution)/shard_map/ppermute | solution.py:51
  411.2 17.3 %collective-permute-start.53 = (f32[2,384]{1,0:T(2,128)S(1)}, f32[2,384]{1,0:T(2,128)S(1)}, u32[]{:S(2)}, u32[]{:S(2)}) collective-permute-start(f32[2,384]{1,0:T(2,128)S(1)} %fusion.24), channel_id=1, source_target_pairs={{0,16},{4,20},{8,24},{12,28},{16,0},{20,4},{24,8},{28,12},{1,17},{... | collective-permute-start | bytes 9224 | tf_op jit(solution)/shard_map/ppermute | solution.py:51
  (105 other events, 790.7 us)
Sparse Core Ops, SparseCore 0:
  30.3 116.6 all-gather.2
  228.7 106.7 reduce-scatter.1
